TPU v7x, 256 devices: a whole 4x4x8 slice. The times are simulated.
256 devices in a mesh: gx: 16 (over x, z_lo), gy: 4 (over z_hi, core), gz: 4 (over y).
Axes of the slice: x: 4, y: 4, z: 8 (z_hi: 2, z_lo: 4; z = z_hi * 4 + z_lo), core: 2. Of those that a mesh axis runs over, the one named last changes fastest.
Arguments:
- point_frac: float32 [3, 1048576], P(None, ('gx', 'gy', 'gz')), may hold values from 0.5 to 1.5
- cell_offset: int32 [3, 1048576], P(None, ('gx', 'gy', 'gz')), may hold values from 0 to 3
- point_velocity: float32 [3, 1048576], P(None, ('gx', 'gy', 'gz')), may hold values from -6 to 6
- point_affine: float32 [9, 1048576], P(None, ('gx', 'gy', 'gz')), may hold values from -3 to 3
- point_stress: float32 [6, 1048576], P(None, ('gx', 'gy', 'gz')), may hold values from -9.5 to 3, as said below
- point_mass: float32 [1048576], P(('gx', 'gy', 'gz')), may hold values from 0.5 to 2
- block_tile: int32 [8192], P(('gx', 'gy', 'gz')), may hold values from 0 to 511, as said below
- block_count: int32 [8192], P(('gx', 'gy', 'gz')), may hold values from 1 to 128, as said below
Outputs:
- new_velocity: float32 [3, 1048576], P(None, ('gx', 'gy', 'gz'))
- new_affine: float32 [9, 1048576], P(None, ('gx', 'gy', 'gz'))
- new_stress: float32 [6, 1048576], P(None, ('gx', 'gy', 'gz'))
- grid_velocity: float32 [3, 256, 256, 128], P(None, 'gx', 'gy', 'gz')
Inputs may be any that keep to these rules, and one draw needn't show every extreme that they name: `block_tile`: block b lies on the device numbered b // 32 (gz fastest, then gy, then gx) and names a tile of that device's region, t = (tx 64 / 4 + ty) * 8 + tz; a tile may be named by no block or by several. The first block_count slots of a block hold live points. `point_stress`: components in the order xx, yy, zz, yz, xz, xy.
All inputs are finite; a program needn't handle non-finite values.
Results may differ from a plain program's by a relative error of at most 0.0003.
Values sent between devices are 32-bit elements; how exact they have to be, the bound alone decides.
A program may use at most 128 MiB of HBM per device.

v0:
```python
import jax
import jax.numpy as jnp
from jax import lax
from jax.experimental import pallas as pl
from jax.experimental.pallas import tpu as pltpu
from jax.sharding import PartitionSpec as P

CX = 16
CY = 64
CZ = 32
BLOCK = 128

time_step = 0.1
gravity = 1.0
shear_modulus = 2.0
bulk_modulus = 4.0
friction_static = 0.38
friction_limit = 0.64
inertial_ref = 0.28
grain_size = 0.5
grain_density = 1.0
pressure_floor = 0.5
shear_floor = 0.5
mass_floor = 0.05
stress_scale = 0.4
pair_index = ((0, 5, 4), (5, 1, 3), (4, 3, 2))
component_pairs = ((0, 0), (1, 1), (2, 2), (1, 2), (0, 2), (0, 1))

PX = CX + 2
PY = 72
PITCH = 40
LANES = 128
ROWS = PX * PY
MESH = pl.DeviceIdType.MESH

T_WX, T_WXD = 0, 6
T_LY, T_MY, T_RY, T_OY, T_Y = 12, 13, 14, 15, 16
T_LZ, T_MZ, T_RZ, T_OZ, T_Z = 17, 18, 19, 20, 21
T_SHARED = 22
T_MASS, T_MV, T_A = 22, 23, 26
T_ALL = 35


def stress_update(stress, affine):
    strain_rate = [
        [
            0.5 * (affine[3 * row_dim + col_dim] + affine[3 * col_dim + row_dim])
            for col_dim in range(3)
        ]
        for row_dim in range(3)
    ]
    volume_rate = strain_rate[0][0] + strain_rate[1][1] + strain_rate[2][2]
    deviator = [
        [
            strain_rate[row_dim][col_dim] - (volume_rate / 3.0 if row_dim == col_dim else 0.0)
            for col_dim in range(3)
        ]
        for row_dim in range(3)
    ]
    trial_stress = []
    for component in range(6):
        row_dim, col_dim = component_pairs[component]
        value = stress[component] + time_step * 2.0 * shear_modulus * deviator[row_dim][col_dim]
        if component < 3:
            value = value + time_step * bulk_modulus * volume_rate
        trial_stress.append(value)
    pressure = -(trial_stress[0] + trial_stress[1] + trial_stress[2]) / 3.0
    shear_part = [trial_stress[component] + pressure for component in range(3)] + trial_stress[3:]
    shear_stress = jnp.sqrt(
        0.5 * (shear_part[0] ** 2 + shear_part[1] ** 2 + shear_part[2] ** 2)
        + shear_part[3] ** 2
        + shear_part[4] ** 2
        + shear_part[5] ** 2
    )
    shear_rate = jnp.sqrt(
        2.0
        * (
            deviator[0][0] ** 2
            + deviator[1][1] ** 2
            + deviator[2][2] ** 2
            + 2.0 * (deviator[1][2] ** 2 + deviator[0][2] ** 2 + deviator[0][1] ** 2)
        )
    )
    inertial = (
        shear_rate * grain_size / jnp.sqrt(jnp.maximum(pressure, pressure_floor) / grain_density)
    )
    friction = friction_static + (friction_limit - friction_static) * inertial / (
        inertial_ref + inertial
    )
    support = jnp.maximum(pressure, 0.0)
    factor = jnp.minimum(1.0, friction * support / jnp.maximum(shear_stress, shear_floor))
    return [shear_part[component] * factor - support for component in range(3)] + [
        shear_part[component] * factor for component in range(3, 6)
    ]


def split(values):
    high = values.astype(jnp.bfloat16)
    low = (values - high.astype(jnp.float32)).astype(jnp.bfloat16)
    return high, low


def tile_coords(tile_ref, block):
    tile = tile_ref[block]
    return tile // 128, (tile // 8) % 16, tile % 8


def axis_weights(row, left, middle, right, offset, position):
    index = lax.broadcasted_iota(jnp.int32, (8, LANES), 0).astype(jnp.float32)
    shifted = index - row(offset)
    weight = jnp.where(
        shifted == 0.0,
        row(left),
        jnp.where(shifted == 1.0, row(middle), jnp.where(shifted == 2.0, row(right), 0.0)),
    )
    return weight, weight * (index - row(position))


def deposit_kernel(
    tile_ref,
    count_ref,
    frac_ref,
    offset_ref,
    velocity_ref,
    affine_ref,
    stress_ref,
    mass_ref,
    new_stress_ref,
    mom_ref,
    grid_mass_ref,
    shared_ref,
    gathered,
    table,
    stress_out,
):
    blocks = mass_ref.shape[0]
    lane = lax.broadcasted_iota(jnp.int32, (1, LANES), 1)
    stride = 48
    for block in range(blocks):
        cols = slice(block * BLOCK, (block + 1) * BLOCK)
        at = block * stride
        gathered[at : at + 3, :] = frac_ref[:, cols]
        gathered[at + 8 : at + 11, :] = offset_ref[:, cols].astype(jnp.float32)
        gathered[at + 16 : at + 19, :] = velocity_ref[:, cols]
        gathered[at + 24 : at + 33, :] = affine_ref[:, cols]
        gathered[at + 40 : at + 46, :] = stress_ref[:, cols]
        row = T_MASS * blocks + block
        table[row : row + 1, :] = jnp.where(
            lane < count_ref[block], mass_ref[block : block + 1, :], 0.0
        )

    def dense(component):
        return gathered[pl.ds(component, blocks, stride=stride), :]

    def put(index, value):
        table[index * blocks : (index + 1) * blocks, :] = value

    affine = [dense(24 + component) for component in range(9)]
    stress = stress_update([dense(40 + component) for component in range(6)], affine)
    for component in range(6):
        stress_out[component * blocks : (component + 1) * blocks, :] = stress[component]
    live_mass = table[T_MASS * blocks : (T_MASS + 1) * blocks, :]
    for row_dim in range(3):
        put(T_MV + row_dim, live_mass * dense(16 + row_dim))
        for col_dim in range(3):
            put(
                T_A + 3 * row_dim + col_dim,
                live_mass
                * (
                    affine[3 * row_dim + col_dim]
                    - stress_scale * stress[pair_index[row_dim][col_dim]]
                ),
            )
    spline = []
    for dim in range(3):
        fraction = dense(dim)
        spline.append(
            (
                0.5 * (1.5 - fraction) ** 2,
                0.75 - (fraction - 1.0) ** 2,
                0.5 * (fraction - 0.5) ** 2,
                dense(8 + dim),
                dense(8 + dim) + fraction,
            )
        )
    left, middle, right, offset, position = spline[0]
    for node in range(6):
        shifted = float(node) - offset
        weight = jnp.where(
            shifted == 0.0,
            left,
            jnp.where(shifted == 1.0, middle, jnp.where(shifted == 2.0, right, 0.0)),
        )
        put(T_WX + node, weight)
        put(T_WXD + node, weight * (float(node) - position))
    for index in range(5):
        put(T_LY + index, spline[1][index])
        put(T_LZ + index, spline[2][index])
    shared_ref[...] = table[: T_SHARED * blocks, :]
    for block in range(blocks):
        new_stress_ref[:, block * BLOCK : (block + 1) * BLOCK] = stress_out[
            pl.ds(block, 6, stride=blocks), :
        ]
    mom_ref[...] = jnp.zeros_like(mom_ref)
    grid_mass_ref[...] = jnp.zeros_like(grid_mass_ref)

    lanes = lax.broadcasted_iota(jnp.int32, (8, LANES), 1)
    gap = jnp.zeros((PITCH - 8, LANES), jnp.float32)
    blank = jnp.zeros((8, LANES), jnp.float32)

    def one(block, carry):
        def row(index):
            return jnp.broadcast_to(table[pl.ds(index * blocks + block, 1), :], (8, LANES))

        wy, wyd = axis_weights(row, T_LY, T_MY, T_RY, T_OY, T_Y)
        wz, wzd = axis_weights(row, T_LZ, T_MZ, T_RZ, T_OZ, T_Z)
        wx = [row(T_WX + node) for node in range(6)]
        wxd = [row(T_WXD + node) for node in range(6)]
        left_side = jnp.concatenate(
            [
                jnp.concatenate([w * wy for w in wx], axis=0),
                jnp.concatenate([w * wy for w in wxd], axis=0),
                jnp.concatenate([w * wyd for w in wx], axis=0),
            ],
            axis=1,
        )
        value_rows = [
            wz * row(T_MV + dim) + wzd * row(T_A + 3 * dim + 2) for dim in range(3)
        ] + [wz * row(T_MASS)]
        x_rows = [wz * row(T_A + 3 * dim) for dim in range(3)] + [blank]
        y_rows = [wz * row(T_A + 3 * dim + 1) for dim in range(3)] + [blank]
        right_side = jnp.concatenate(
            [
                jnp.concatenate([r[0], gap, r[1], gap, r[2], gap, r[3]], axis=0)
                for r in (value_rows, x_rows, y_rows)
            ],
            axis=1,
        )
        left_high, left_low = split(left_side)
        right_high, right_low = split(right_side)

        def product(a, b):
            return lax.dot_general(
                a, b, (((1,), (1,)), ((), ())), preferred_element_type=jnp.float32
            )

        sums = (
            product(left_high, right_high)
            + product(left_high, right_low)
            + product(left_low, right_high)
        )
        tile_x, tile_y, tile_z = tile_coords(tile_ref, block)
        for node in range(6):
            part = sums[8 * node : 8 * node + 8]
            at = pl.ds(pl.multiple_of((4 * tile_x + node) * PY + 4 * tile_y, 4), 8)
            mom_ref[at, :] += pltpu.roll(
                jnp.where(lanes < 3 * PITCH, part, 0.0), 4 * tile_z, axis=1
            )
            grid_mass_ref[at, :] += pltpu.roll(
                jnp.where(lanes >= 3 * PITCH, part, 0.0), 8 + 4 * tile_z, axis=1
            )
        return carry

    lax.fori_loop(0, blocks, one, 0)


def exchange_kernel(
    mom_in,
    mass_in,
    mom,
    mass,
    z_send,
    z_recv,
    xm_recv,
    xs_send,
    xs_recv,
    y_send,
    y_recv,
    e_send,
    e_recv,
    send_sem,
    recv_sem,
):
    axes = ("gx", "gy", "gz")
    me = {axis: lax.axis_index(axis) for axis in axes}
    count = {axis: lax.axis_size(axis) for axis in axes}

    def device(dx, dy, dz):
        return tuple(
            lax.rem(me[axis] + count[axis] + step, count[axis])
            for axis, step in zip(axes, (dx, dy, dz))
        )

    z_steps = [(0, 0, -1), (0, 0, 1)]
    x_steps = [(-1, 0, 0), (1, 0, 0)]
    y_steps = [(0, -1, 0), (0, 1, 0)]
    e_steps = [(-1, -1, 0), (-1, 1, 0), (1, -1, 0), (1, 1, 0)]
    barrier = pltpu.get_barrier_semaphore()
    for step in z_steps + x_steps + y_steps + e_steps:
        pl.semaphore_signal(barrier, inc=1, device_id=device(*step), device_id_type=MESH)

    def copy(src, dst, slot, step):
        return pltpu.make_async_remote_copy(
            src_ref=src,
            dst_ref=dst,
            send_sem=send_sem.at[slot],
            recv_sem=recv_sem.at[slot],
            device_id=device(*step),
            device_id_type=MESH,
        )

    lane = lax.broadcasted_iota(jnp.int32, (PY, LANES), 1)
    in_mom = lane < 3 * PITCH
    in_pitch = lax.rem(lane, PITCH)
    third = PY // 3
    lane3 = lane[:third]
    in_pitch3 = in_pitch[:third]
    in_mom3 = in_mom[:third]

    for side in range(2):
        shift = 0 if side == 0 else LANES - CZ

        def pack(x, carry):
            packed, packed_mass = carry
            at = pl.ds(pl.multiple_of(x * PY, 8), PY)
            mine = (in_pitch >= 2 * x) & (in_pitch < 2 * x + 2) & in_mom
            packed = jnp.where(
                mine, pltpu.roll(mom_in[at, :], lax.rem(2 * x + shift, LANES), axis=1), packed
            )
            layer = mass_in[at, :]
            for group in range(3):
                start = PITCH * group
                here = (lane3 >= start + 2 * x) & (lane3 < start + 2 * x + 2)
                packed_mass = jnp.where(
                    here,
                    pltpu.roll(
                        layer[group * third : (group + 1) * third],
                        lax.rem(start + 2 * x + shift, LANES),
                        axis=1,
                    ),
                    packed_mass,
                )
            return packed, packed_mass

        packed, packed_mass = lax.fori_loop(
            0,
            PX,
            pack,
            (jnp.zeros((PY, LANES), jnp.float32), jnp.zeros((third, LANES), jnp.float32)),
        )
        z_send[side, :PY, :] = packed
        z_send[side, PY:, :] = packed_mass

    pl.semaphore_wait(barrier, 10)
    z_copies = [
        copy(z_send.at[side], z_recv.at[1 - side], side, z_steps[side]) for side in range(2)
    ]
    for c in z_copies:
        c.start()
    for c in z_copies:
        c.wait()

    low = (in_pitch < 2) & in_mom
    high = (in_pitch >= CZ) & (in_pitch < CZ + 2) & in_mom
    low3 = lane3 < 2
    high3 = (lane3 >= CZ) & (lane3 < CZ + 2)

    def unpack(x, carry):
        at = pl.ds(pl.multiple_of(x * PY, 8), PY)
        from_low = pltpu.roll(z_recv[0, :PY, :], lax.rem(LANES - 2 * x, LANES), axis=1)
        from_high = pltpu.roll(z_recv[1, :PY, :], lax.rem(LANES + CZ - 2 * x, LANES), axis=1)
        mom[at, :] = (
            mom_in[at, :] + jnp.where(low, from_low, 0.0) + jnp.where(high, from_high, 0.0)
        )
        for group in range(3):
            start = PITCH * group
            rows = pl.ds(pl.multiple_of(x * PY + group * third, 8), third)
            from_low = pltpu.roll(
                z_recv[0, PY:, :], lax.rem(2 * LANES - start - 2 * x, LANES), axis=1
            )
            from_high = pltpu.roll(
                z_recv[1, PY:, :], lax.rem(2 * LANES + CZ - start - 2 * x, LANES), axis=1
            )
            mass[rows, :] = (
                mass_in[rows, :]
                + jnp.where(low3, from_low, 0.0)
                + jnp.where(high3, from_high, 0.0)
            )
        return carry

    lax.fori_loop(0, PX, unpack, 0)

    firsts = (0, CX)
    y_firsts = (0, CY)
    copies = []
    for side in range(2):
        first = firsts[side] * PY
        xs_send[side] = mass[first : first + PY, :] + pltpu.roll(
            mass[first + PY : first + 2 * PY, :], 64, axis=1
        )
        copies.append(
            copy(
                mom.at[pl.ds(first, 2 * PY), :], xm_recv.at[1 - side], 2 + side, x_steps[side]
            )
        )
        copies.append(copy(xs_send.at[side], xs_recv.at[1 - side], 4 + side, x_steps[side]))
    for c in copies:
        c.start()
    more = []
    for side in range(2):
        y0 = y_firsts[side]
        y_send[side, 0:PX, :] = mom[pl.ds(y0, PX, stride=PY), :]
        y_send[side, 24 : 24 + PX, :] = mom[pl.ds(y0 + 1, PX, stride=PY), :]
        y_send[side, 48 : 48 + PX, :] = mass[pl.ds(y0, PX, stride=PY), :] + pltpu.roll(
            mass[pl.ds(y0 + 1, PX, stride=PY), :], 64, axis=1
        )
        y_send[side, PX:24, :] = jnp.zeros((24 - PX, LANES), jnp.float32)
        y_send[side, 24 + PX : 48, :] = jnp.zeros((24 - PX, LANES), jnp.float32)
        y_send[side, 48 + PX : 72, :] = jnp.zeros((24 - PX, LANES), jnp.float32)
        more.append(copy(y_send.at[side], y_recv.at[1 - side], 6 + side, y_steps[side]))
    for edge in range(4):
        x0, y0 = firsts[edge // 2], y_firsts[edge % 2]
        for layer in range(2):
            at = (x0 + layer) * PY + y0
            e_send[edge, 2 * layer : 2 * layer + 2, :] = mom[at : at + 2, :]
            e_send[edge, 4 + 2 * layer : 6 + 2 * layer, :] = mass[at : at + 2, :]
        more.append(copy(e_send.at[edge], e_recv.at[3 - edge], 8 + edge, e_steps[edge]))
    for c in more:
        c.start()
    for c in copies + more:
        c.wait()
    front = lane < 64
    front_x = lax.broadcasted_iota(jnp.int32, (PX, LANES), 1) < 64
    for side in range(2):
        first = firsts[side] * PY
        mom[first : first + 2 * PY, :] += xm_recv[side]
        got = xs_recv[side]
        mass[first : first + PY, :] += jnp.where(front, got, 0.0)
        mass[first + PY : first + 2 * PY, :] += jnp.where(
            front, pltpu.roll(got, 64, axis=1), 0.0
        )
    for side in range(2):
        y0 = y_firsts[side]
        got = y_recv[side, 48 : 48 + PX, :]
        at0 = pl.ds(y0, PX, stride=PY)
        at1 = pl.ds(y0 + 1, PX, stride=PY)
        mom[at0, :] = mom[at0, :] + y_recv[side, 0:PX, :]
        mom[at1, :] = mom[at1, :] + y_recv[side, 24 : 24 + PX, :]
        mass[at0, :] = mass[at0, :] + jnp.where(front_x, got, 0.0)
        mass[at1, :] = mass[at1, :] + jnp.where(front_x, pltpu.roll(got, 64, axis=1), 0.0)
    for edge in range(4):
        x0, y0 = firsts[edge // 2], y_firsts[edge % 2]
        for layer in range(2):
            at = (x0 + layer) * PY + y0
            mom[at : at + 2, :] += e_recv[edge, 2 * layer : 2 * layer + 2, :]
            mass[at : at + 2, :] += e_recv[edge, 4 + 2 * layer : 6 + 2 * layer, :]


def collect_kernel(
    tile_ref,
    mom_ref,
    mass_ref,
    shared_ref,
    new_velocity_ref,
    new_affine_ref,
    grid_velocity_ref,
    velocity,
    partial,
    final,
):
    blocks = tile_ref.shape[0]
    width_x = lax.axis_size("gx") * CX
    height_y = lax.axis_size("gy") * CY
    depth_z = lax.axis_size("gz") * CZ
    lane = lax.broadcasted_iota(jnp.int32, (PY, LANES), 1)
    row_index = lax.broadcasted_iota(jnp.int32, (PY, LANES), 0)
    first_z = lax.axis_index("gz") * CZ
    first_y = lax.axis_index("gy") * CY
    first_x = lax.axis_index("gx") * CX
    z_index = lax.rem(lane - 2 * PITCH - 1 + first_z + depth_z, depth_z)
    y_index = lax.rem(row_index - 1 + first_y + height_y, height_y)
    is_y = (lane >= PITCH) & (lane < 2 * PITCH)
    is_z = (lane >= 2 * PITCH) & (lane < 3 * PITCH)
    z_floor = is_z & (z_index < 2)
    z_top = is_z & (z_index >= depth_z - 2)
    y_floor = is_y & (y_index < 2)
    fall = jnp.where(is_y, time_step * gravity, 0.0)

    def layer(x, carry):
        at = pl.ds(pl.multiple_of(x * PY, 8), PY)
        x_index = lax.rem(first_x + x - 1 + width_x, width_x)
        outlet = (x_index >= width_x // 4) & (x_index < width_x - width_x // 4)
        inverse = 1.0 / (mass_ref[at, :] + mass_floor)
        inverse = jnp.where(
            lane < PITCH,
            inverse,
            jnp.where(
                is_y, pltpu.roll(inverse, PITCH, axis=1), pltpu.roll(inverse, 2 * PITCH, axis=1)
            ),
        )
        values = mom_ref[at, :] * inverse - fall
        lifted = jnp.maximum(values, 0.0)
        values = jnp.where(
            z_floor | (y_floor & jnp.logical_not(outlet)), lifted, values
        )
        values = jnp.where(z_top, jnp.minimum(values, 0.0), values)
        velocity[at, :] = values
        return carry

    lax.fori_loop(0, PX, layer, 0)

    def output(x, carry):
        rows = velocity[pl.ds((x + 1) * PY + 1, CY), :]
        for dim in range(3):
            grid_velocity_ref[dim, x] = pltpu.roll(
                rows, LANES - PITCH * dim - 1, axis=1
            )[:, :CZ]
        return carry

    lax.fori_loop(0, CX, output, 0)

    lanes = lax.broadcasted_iota(jnp.int32, (8, LANES), 1)

    def one(block, carry):
        def row(index):
            return jnp.broadcast_to(shared_ref[pl.ds(index * blocks + block, 1), :], (8, LANES))

        wy, wyd = axis_weights(row, T_LY, T_MY, T_RY, T_OY, T_Y)
        wz, wzd = axis_weights(row, T_LZ, T_MZ, T_RZ, T_OZ, T_Z)
        wx = [row(T_WX + node) for node in range(6)]
        wxd = [row(T_WXD + node) for node in range(6)]
        right_side = jnp.concatenate(
            [
                jnp.concatenate([w * wz for w in wx], axis=0),
                jnp.concatenate([w * wz for w in wxd], axis=0),
                jnp.concatenate([w * wzd for w in wx], axis=0),
            ],
            axis=1,
        )
        tile_x, tile_y, tile_z = tile_coords(tile_ref, block)
        planes = []
        for node in range(6):
            at = pl.ds(pl.multiple_of((4 * tile_x + node) * PY + 4 * tile_y, 4), 8)
            planes.append(velocity[at, :])
        rows = []
        for dim in range(3):
            merged = None
            for node in range(6):
                moved = pltpu.roll(
                    planes[node],
                    lax.rem(2 * LANES + 8 * node - PITCH * dim - 4 * tile_z, LANES),
                    axis=1,
                )
                merged = moved if merged is None else jnp.where(lanes < 8 * node, merged, moved)
            rows.append(merged)
        left_side = jnp.concatenate(rows, axis=0)[:, :48]
        left_high, left_low = split(left_side)
        right_high, right_low = split(right_side)
        sums = (
            jnp.dot(left_high, right_high, preferred_element_type=jnp.float32)
            + jnp.dot(left_high, right_low, preferred_element_type=jnp.float32)
            + jnp.dot(left_low, right_high, preferred_element_type=jnp.float32)
        )
        for dim in range(3):
            part = sums[8 * dim : 8 * dim + 8]
            terms = (
                (dim, wy * part[:, :128]),
                (3 + 3 * dim, wy * part[:, 128:256]),
                (4 + 3 * dim, wyd * part[:, :128]),
                (5 + 3 * dim, wy * part[:, 256:]),
            )
            for component, value in terms:
                at = pl.ds(pl.multiple_of(component * 8 * blocks + 8 * block, 8), 8)
                partial[at, :] = value
        return carry

    lax.fori_loop(0, blocks, one, 0)
    for component in range(12):
        total = partial[pl.ds(component * 8 * blocks, blocks, stride=8), :]
        for node in range(1, 6):
            total = total + partial[pl.ds(component * 8 * blocks + node, blocks, stride=8), :]
        if component >= 3:
            total = 4.0 * total
        final[component * blocks : (component + 1) * blocks, :] = total
    for block in range(blocks):
        cols = slice(block * BLOCK, (block + 1) * BLOCK)
        new_velocity_ref[:, cols] = final[pl.ds(block, 3, stride=blocks), :]
        new_affine_ref[:, cols] = final[pl.ds(3 * blocks + block, 9, stride=blocks), :]


def shards(
    point_frac,
    cell_offset,
    point_velocity,
    point_affine,
    point_stress,
    point_mass,
    block_tile,
    block_count,
):
    blocks = block_tile.shape[0]
    points = blocks * BLOCK
    vmem = pl.BlockSpec(memory_space=pltpu.VMEM)
    smem = pl.BlockSpec(memory_space=pltpu.SMEM)
    f32 = jnp.float32
    grid_shape = jax.ShapeDtypeStruct((ROWS, LANES), f32)
    new_stress, mom, mass, shared = pl.pallas_call(
        deposit_kernel,
        name="deposit",
        out_shape=(
            jax.ShapeDtypeStruct((6, points), f32),
            grid_shape,
            grid_shape,
            jax.ShapeDtypeStruct((T_SHARED * blocks, LANES), f32),
        ),
        in_specs=[smem, smem] + [vmem] * 6,
        out_specs=(vmem,) * 4,
        scratch_shapes=[
            pltpu.VMEM((48 * blocks, LANES), f32),
            pltpu.VMEM((T_ALL * blocks, LANES), f32),
            pltpu.VMEM((8 * blocks, LANES), f32),
        ],
    )(
        block_tile,
        block_count,
        point_frac,
        cell_offset,
        point_velocity,
        point_affine,
        point_stress,
        point_mass.reshape(blocks, BLOCK),
    )
    mom, mass = pl.pallas_call(
        exchange_kernel,
        name="exchange",
        out_shape=(grid_shape, grid_shape),
        in_specs=[vmem] * 2,
        out_specs=(vmem,) * 2,
        scratch_shapes=[
            pltpu.VMEM((2, PY + PY // 3, LANES), f32),
            pltpu.VMEM((2, PY + PY // 3, LANES), f32),
            pltpu.VMEM((2, 2 * PY, LANES), f32),
            pltpu.VMEM((2, PY, LANES), f32),
            pltpu.VMEM((2, PY, LANES), f32),
            pltpu.VMEM((2, 72, LANES), f32),
            pltpu.VMEM((2, 72, LANES), f32),
            pltpu.VMEM((4, 8, LANES), f32),
            pltpu.VMEM((4, 8, LANES), f32),
            pltpu.SemaphoreType.DMA((12,)),
            pltpu.SemaphoreType.DMA((12,)),
        ],
        compiler_params=pltpu.CompilerParams(collective_id=0, has_side_effects=True),
    )(mom, mass)
    new_velocity, new_affine, grid_velocity = pl.pallas_call(
        collect_kernel,
        name="collect",
        out_shape=(
            jax.ShapeDtypeStruct((3, points), f32),
            jax.ShapeDtypeStruct((9, points), f32),
            jax.ShapeDtypeStruct((3, CX, CY, CZ), f32),
        ),
        in_specs=[smem] + [vmem] * 3,
        out_specs=(vmem,) * 3,
        scratch_shapes=[
            pltpu.VMEM((ROWS, LANES), f32),
            pltpu.VMEM((12 * 8 * blocks, LANES), f32),
            pltpu.VMEM((12 * blocks, LANES), f32),
        ],
    )(block_tile, mom, mass, shared)
    return (new_velocity, new_affine, new_stress, grid_velocity)


def solution(mesh):
    points = P(None, ("gx", "gy", "gz"))
    flat = P(("gx", "gy", "gz"))
    return jax.shard_map(
        shards,
        mesh=mesh,
        in_specs=(points,) * 5 + (flat,) * 3,
        out_specs=(points, points, points, P(None, "gx", "gy", "gz")),
        check_vma=False,
    )
```

profile of v0, /device:TPU:1, one launch (start us, length us, event | category | flops | bytes accessed | tf_op | source)
XLA Modules:
  0.0 60.3 jit_solution(1094427845149313463)
XLA Ops:
  0.6 12.9 %deposit.1 = (f32[6,4096]{1,0:T(8,128)}, f32[1296,128]{1,0:T(8,128)}, f32[1296,128]{1,0:T(8,128)}, f32[704,128]{1,0:T(8,128)}) custom-call(s32[32]{0:T(128)} %tile_ref.3, s32[32]{0:T(128)} %count_ref.1, f32[3,4096]{1,0:T(4,128)} %frac_ref.1, s32[3,4096]{1,0:T(4,128)} %offset_ref.1, f32[3,4096]{1,0:T(4,128)} %velocity_ref.1, f32[9,4096]{1,0:T(8,128)} %affine_ref.1, ...), custom_call_target="tpu_custom_call" | custom-call | tf_op jit(solution)/shard_map/deposit/pallas_call | solution.py:607
  13.5 29.4 %exchange.1 = (f32[1296,128]{1,0:T(8,128)}, f32[1296,128]{1,0:T(8,128)}) custom-call(f32[1296,128]{1,0:T(8,128)} %get-tuple-element.13.mom_in, f32[1296,128]{1,0:T(8,128)} %get-tuple-element.14.mass_in), custom_call_target="tpu_custom_call" | custom-call | tf_op jit(solution)/shard_map/exchange/pallas_call | solution.py:633
  43.0 14.6 %collect.1 = (f32[3,4096]{1,0:T(4,128)}, f32[9,4096]{1,0:T(8,128)}, f32[3,16,64,32]{3,2,1,0:T(8,128)}) custom-call(s32[32]{0:T(128)} %tile_ref.3, f32[1296,128]{1,0:T(8,128)} %get-tuple-element.15.mom_ref, f32[1296,128]{1,0:T(8,128)} %get-tuple-element.16.mass_ref, f32[704,128]{1,0:T(8,128)} %get-tuple-element.17.shared_ref), custom_call_target="tpu_custom_call" | custom-call | tf_op jit(solution)/shard_map/collect/pallas_call | solution.py:654
  57.5 2.7 %copy.12 = f32[3,16,64,32]{2,3,1,0:T(8,128)} copy(f32[3,16,64,32]{3,2,1,0:T(8,128)} %get-tuple-element.25) | data formatting | bytes 786432
where the time goes:
time: 60.5 us; the launch traced here: 60.3 us
  Pallas kernels  56.9 us (94%)
  local copies, waits for them, and re-layouts  2.75 us (5%)
  between operations  0.64 us (1%)
    pallas_call x1, Pallas kernels, shards(): pl.pallas_call(exchange_kernel, name='exchange', out_shape=(grid_shape, g...  29.4 us
    pallas_call x1, Pallas kernels, shards(): pl.pallas_call(collect_kernel, name='collect', out_shape=(jax.ShapeDtypeS...  14.6 us
    pallas_call x1, Pallas kernels, shards(): pl.pallas_call(deposit_kernel, name='deposit', out_shape=(jax.ShapeDtypeS...  12.9 us
    unnamed x1, local copies, waits for them, and re-layouts  2.75 us

commit v1 on v0

--- a/solution.py
+++ b/solution.py
@@ -31,6 +31,8 @@
 PITCH = 40
 LANES = 128
 ROWS = PX * PY
+GROUP = 4
+VMEM_LIMIT = 16 * 1024 * 1024
 MESH = pl.DeviceIdType.MESH
 
 T_WX, T_WXD = 0, 6
@@ -102,7 +104,7 @@
 
 def tile_coords(tile_ref, block):
     tile = tile_ref[block]
-    return tile // 128, (tile // 8) % 16, tile % 8
+    return tile >> 7, (tile >> 3) & 15, tile & 7
 
 
 def axis_weights(row, left, middle, right, offset, position):
@@ -204,11 +206,12 @@
     mom_ref[...] = jnp.zeros_like(mom_ref)
     grid_mass_ref[...] = jnp.zeros_like(grid_mass_ref)
 
-    lanes = lax.broadcasted_iota(jnp.int32, (8, LANES), 1)
-    gap = jnp.zeros((PITCH - 8, LANES), jnp.float32)
+    lanes = lax.broadcasted_iota(jnp.int32, (8, 32), 1)
+    channel = [(lanes >= 8 * index) & (lanes < 8 * index + 8) for index in range(4)]
+    rest = jnp.zeros((8, LANES - 32), jnp.float32)
     blank = jnp.zeros((8, LANES), jnp.float32)
 
-    def one(block, carry):
+    def block_sums(block):
         def row(index):
             return jnp.broadcast_to(table[pl.ds(index * blocks + block, 1), :], (8, LANES))
 
@@ -230,11 +233,7 @@
         x_rows = [wz * row(T_A + 3 * dim) for dim in range(3)] + [blank]
         y_rows = [wz * row(T_A + 3 * dim + 1) for dim in range(3)] + [blank]
         right_side = jnp.concatenate(
-            [
-                jnp.concatenate([r[0], gap, r[1], gap, r[2], gap, r[3]], axis=0)
-                for r in (value_rows, x_rows, y_rows)
-            ],
-            axis=1,
+            [jnp.concatenate(r, axis=0) for r in (value_rows, x_rows, y_rows)], axis=1
         )
         left_high, left_low = split(left_side)
         right_high, right_low = split(right_side)
@@ -244,24 +243,49 @@
                 a, b, (((1,), (1,)), ((), ())), preferred_element_type=jnp.float32
             )
 
-        sums = (
+        return (
             product(left_high, right_high)
             + product(left_high, right_low)
             + product(left_low, right_high)
         )
+
+    def scatter(block, sums):
         tile_x, tile_y, tile_z = tile_coords(tile_ref, block)
+        starts = (0, PITCH - 8, 2 * PITCH - 16, LANES - 24)
+        places, moved = [], []
         for node in range(6):
             part = sums[8 * node : 8 * node + 8]
-            at = pl.ds(pl.multiple_of((4 * tile_x + node) * PY + 4 * tile_y, 4), 8)
-            mom_ref[at, :] += pltpu.roll(
-                jnp.where(lanes < 3 * PITCH, part, 0.0), 4 * tile_z, axis=1
-            )
-            grid_mass_ref[at, :] += pltpu.roll(
-                jnp.where(lanes >= 3 * PITCH, part, 0.0), 8 + 4 * tile_z, axis=1
-            )
-        return carry
-
-    lax.fori_loop(0, blocks, one, 0)
+            places.append(pl.ds(pl.multiple_of((4 * tile_x + node) * PY + 4 * tile_y, 4), 8))
+            moved.append(
+                [
+                    pltpu.roll(
+                        jnp.concatenate([jnp.where(channel[index], part, 0.0), rest], axis=1),
+                        starts[index] + 4 * tile_z,
+                        axis=1,
+                    )
+                    for index in range(4)
+                ]
+            )
+        mom = [mom_ref[at, :] for at in places]
+        mass = [grid_mass_ref[at, :] for at in places]
+        for node, at in enumerate(places):
+            mom_ref[at, :] = mom[node] + moved[node][0] + moved[node][1] + moved[node][2]
+            grid_mass_ref[at, :] = mass[node] + moved[node][3]
+
+    def group_sums(step):
+        return tuple(block_sums(step * GROUP + member) for member in range(GROUP))
+
+    def group_scatter(step, sums):
+        for member in range(GROUP):
+            scatter(step * GROUP + member, sums[member])
+
+    def group(step, sums):
+        following = group_sums(step)
+        group_scatter(step - 1, sums)
+        return following
+
+    steps = blocks // GROUP
+    group_scatter(steps - 1, lax.fori_loop(1, steps, group, group_sums(0)))
 
 
 def exchange_kernel(
@@ -486,7 +510,7 @@
     y_floor = is_y & (y_index < 2)
     fall = jnp.where(is_y, time_step * gravity, 0.0)
 
-    def layer(x, carry):
+    def layer(x):
         at = pl.ds(pl.multiple_of(x * PY, 8), PY)
         x_index = lax.rem(first_x + x - 1 + width_x, width_x)
         outlet = (x_index >= width_x // 4) & (x_index < width_x - width_x // 4)
@@ -505,38 +529,33 @@
         )
         values = jnp.where(z_top, jnp.minimum(values, 0.0), values)
         velocity[at, :] = values
+
+    def layers(step, carry):
+        for member in range(3):
+            layer(3 * step + member)
         return carry
 
-    lax.fori_loop(0, PX, layer, 0)
-
-    def output(x, carry):
-        rows = velocity[pl.ds((x + 1) * PY + 1, CY), :]
-        for dim in range(3):
-            grid_velocity_ref[dim, x] = pltpu.roll(
-                rows, LANES - PITCH * dim - 1, axis=1
-            )[:, :CZ]
+    lax.fori_loop(0, PX // 3, layers, 0)
+
+    def output(step, carry):
+        for member in range(4):
+            x = 4 * step + member
+            turned = jnp.transpose(velocity[pl.ds((x + 1) * PY + 1, CY), :])
+            for dim in range(3):
+                grid_velocity_ref[dim, x] = turned[PITCH * dim + 1 : PITCH * dim + 1 + CZ]
         return carry
 
-    lax.fori_loop(0, CX, output, 0)
+    lax.fori_loop(0, CX // 4, output, 0)
 
     lanes = lax.broadcasted_iota(jnp.int32, (8, LANES), 1)
 
-    def one(block, carry):
+    def row_of(block):
         def row(index):
             return jnp.broadcast_to(shared_ref[pl.ds(index * blocks + block, 1), :], (8, LANES))
 
-        wy, wyd = axis_weights(row, T_LY, T_MY, T_RY, T_OY, T_Y)
-        wz, wzd = axis_weights(row, T_LZ, T_MZ, T_RZ, T_OZ, T_Z)
-        wx = [row(T_WX + node) for node in range(6)]
-        wxd = [row(T_WXD + node) for node in range(6)]
-        right_side = jnp.concatenate(
-            [
-                jnp.concatenate([w * wz for w in wx], axis=0),
-                jnp.concatenate([w * wz for w in wxd], axis=0),
-                jnp.concatenate([w * wzd for w in wx], axis=0),
-            ],
-            axis=1,
-        )
+        return row
+
+    def gather(block):
         tile_x, tile_y, tile_z = tile_coords(tile_ref, block)
         planes = []
         for node in range(6):
@@ -548,19 +567,41 @@
             for node in range(6):
                 moved = pltpu.roll(
                     planes[node],
-                    lax.rem(2 * LANES + 8 * node - PITCH * dim - 4 * tile_z, LANES),
+                    LANES + 8 * node - PITCH * dim - 4 * tile_z,
                     axis=1,
                 )
                 merged = moved if merged is None else jnp.where(lanes < 8 * node, merged, moved)
             rows.append(merged)
-        left_side = jnp.concatenate(rows, axis=0)[:, :48]
-        left_high, left_low = split(left_side)
+        return jnp.concatenate(rows, axis=0)
+
+    def contract(block, left_side):
+        row = row_of(block)
+        wz, wzd = axis_weights(row, T_LZ, T_MZ, T_RZ, T_OZ, T_Z)
+        wx = [row(T_WX + node) for node in range(6)]
+        wxd = [row(T_WXD + node) for node in range(6)]
+        right_side = jnp.concatenate(
+            [
+                jnp.concatenate([w * wz for w in wx], axis=0),
+                jnp.concatenate([w * wz for w in wxd], axis=0),
+                jnp.concatenate([w * wzd for w in wx], axis=0),
+            ],
+            axis=1,
+        )
+        left_high, left_low = split(left_side[:, :48])
         right_high, right_low = split(right_side)
-        sums = (
-            jnp.dot(left_high, right_high, preferred_element_type=jnp.float32)
+        both = jnp.dot(
+            jnp.concatenate([left_high, left_low], axis=0),
+            right_high,
+            preferred_element_type=jnp.float32,
+        )
+        return (
+            both[:24]
+            + both[24:]
             + jnp.dot(left_high, right_low, preferred_element_type=jnp.float32)
-            + jnp.dot(left_low, right_high, preferred_element_type=jnp.float32)
-        )
+        )
+
+    def weigh(block, sums):
+        wy, wyd = axis_weights(row_of(block), T_LY, T_MY, T_RY, T_OY, T_Y)
         for dim in range(3):
             part = sums[8 * dim : 8 * dim + 8]
             terms = (
@@ -572,9 +613,25 @@
             for component, value in terms:
                 at = pl.ds(pl.multiple_of(component * 8 * blocks + 8 * block, 8), 8)
                 partial[at, :] = value
-        return carry
-
-    lax.fori_loop(0, blocks, one, 0)
+
+    def of_group(function, step, *values):
+        return tuple(
+            function(step * GROUP + member, *(value[member] for value in values))
+            for member in range(GROUP)
+        )
+
+    def group(step, carry):
+        left_sides, sums = carry
+        following = of_group(gather, step + 2)
+        products = of_group(contract, step + 1, left_sides)
+        of_group(weigh, step, sums)
+        return following, products
+
+    steps = blocks // GROUP
+    carry = of_group(gather, 1), of_group(contract, 0, of_group(gather, 0))
+    left_sides, sums = lax.fori_loop(0, steps - 2, group, carry)
+    of_group(weigh, steps - 2, sums)
+    of_group(weigh, steps - 1, of_group(contract, steps - 1, left_sides))
     for component in range(12):
         total = partial[pl.ds(component * 8 * blocks, blocks, stride=8), :]
         for node in range(1, 6):
@@ -620,6 +677,7 @@
             pltpu.VMEM((T_ALL * blocks, LANES), f32),
             pltpu.VMEM((8 * blocks, LANES), f32),
         ],
+        compiler_params=pltpu.CompilerParams(vmem_limit_bytes=VMEM_LIMIT),
     )(
         block_tile,
         block_count,
@@ -649,7 +707,9 @@
             pltpu.SemaphoreType.DMA((12,)),
             pltpu.SemaphoreType.DMA((12,)),
         ],
-        compiler_params=pltpu.CompilerParams(collective_id=0, has_side_effects=True),
+        compiler_params=pltpu.CompilerParams(
+            collective_id=0, has_side_effects=True, vmem_limit_bytes=VMEM_LIMIT
+        ),
     )(mom, mass)
     new_velocity, new_affine, grid_velocity = pl.pallas_call(
         collect_kernel,
@@ -657,7 +717,7 @@
         out_shape=(
             jax.ShapeDtypeStruct((3, points), f32),
             jax.ShapeDtypeStruct((9, points), f32),
-            jax.ShapeDtypeStruct((3, CX, CY, CZ), f32),
+            jax.ShapeDtypeStruct((3, CX, CZ, CY), f32),
         ),
         in_specs=[smem] + [vmem] * 3,
         out_specs=(vmem,) * 3,
@@ -666,8 +726,9 @@
             pltpu.VMEM((12 * 8 * blocks, LANES), f32),
             pltpu.VMEM((12 * blocks, LANES), f32),
         ],
+        compiler_params=pltpu.CompilerParams(vmem_limit_bytes=VMEM_LIMIT),
     )(block_tile, mom, mass, shared)
-    return (new_velocity, new_affine, new_stress, grid_velocity)
+    return (new_velocity, new_affine, new_stress, jnp.swapaxes(grid_velocity, 2, 3))
 
 
 def solution(mesh):

time: 60.5 us -> 43.4 us (0.72)
  Pallas kernels: 56.9 us -> 36.6 us
  local copies, waits for them, and re-layouts: 2.75 us -> 5.74 us
    pallas_call x1, Pallas kernels: 14.6 us -> 5.15 us  [shards(): pl.pallas_call(collect_kernel, name='collect', out_shape=(jax.ShapeDtypeS...]
    pallas_call x1, Pallas kernels: 12.9 us -> 4.33 us  [shards(): pl.pallas_call(deposit_kernel, name='deposit', out_shape=(jax.ShapeDtypeS...]
    unnamed x1 -> x16, local copies, waits for them, and re-layouts: 2.75 us -> 5.74 us
    pallas_call x1, Pallas kernels: 29.4 us -> 27.2 us  [shards(): pl.pallas_call(exchange_kernel, name='exchange', out_shape=(grid_shape, g...]
where the time goes in v1:
time: 43.4 us; the launch traced here: 43 us
  Pallas kernels  36.6 us (84%)
  local copies, waits for them, and re-layouts  5.74 us (13%)
  between operations  0.66 us (2%)
    pallas_call x1, Pallas kernels, shards(): pl.pallas_call(exchange_kernel, name='exchange', out_shape=(grid_shape, g...  27.2 us
    unnamed x16, local copies, waits for them, and re-layouts  5.74 us
    pallas_call x1, Pallas kernels, shards(): pl.pallas_call(collect_kernel, name='collect', out_shape=(jax.ShapeDtypeS...  5.15 us
    pallas_call x1, Pallas kernels, shards(): pl.pallas_call(deposit_kernel, name='deposit', out_shape=(jax.ShapeDtypeS...  4.33 us

profile of v1, /device:TPU:1, one launch (start us, length us, event | category | flops | bytes accessed | tf_op | source)
XLA Modules:
  0.0 43.0 jit_solution(5746347162071267119)
XLA Ops:
  0.6 0.0 copy-start.6
  0.6 0.0 copy-start.7
  0.7 0.6 %copy-done.6 = s32[32]{0:T(128)S(1)} copy-done((s32[32]{0:T(128)S(1)}, s32[32]{0:T(128)}, u32[]{:S(2)}) %copy-start.6) | copy-done | bytes 152
  1.3 0.0 copy-done.7
  1.3 0.0 copy-start
  1.3 0.9 %copy-done = f32[9,4096]{1,0:T(8,128)S(1)} copy-done((f32[9,4096]{1,0:T(8,128)S(1)}, f32[9,4096]{1,0:T(8,128)}, u32[]{:S(2)}) %copy-start) | copy-done | bytes 147480
  2.3 0.0 copy-start.1
  2.3 0.9 %copy-done.1 = f32[6,4096]{1,0:T(8,128)S(1)} copy-done((f32[6,4096]{1,0:T(8,128)S(1)}, f32[6,4096]{1,0:T(8,128)}, u32[]{:S(2)}) %copy-start.1) | copy-done | bytes 98328
  3.2 0.0 copy-start.2
  3.2 0.8 %copy-done.2 = f32[3,4096]{1,0:T(4,128)S(1)} copy-done((f32[3,4096]{1,0:T(4,128)S(1)}, f32[3,4096]{1,0:T(4,128)}, u32[]{:S(2)}) %copy-start.2) | copy-done | bytes 49176
  4.0 0.0 copy-start.3
  4.0 0.8 %copy-done.3 = s32[3,4096]{1,0:T(4,128)S(1)} copy-done((s32[3,4096]{1,0:T(4,128)S(1)}, s32[3,4096]{1,0:T(4,128)}, u32[]{:S(2)}) %copy-start.3) | copy-done | bytes 49176
  4.8 0.0 copy-start.4
  4.8 0.8 %copy-done.4 = f32[3,4096]{1,0:T(4,128)S(1)} copy-done((f32[3,4096]{1,0:T(4,128)S(1)}, f32[3,4096]{1,0:T(4,128)}, u32[]{:S(2)}) %copy-start.4) | copy-done | bytes 49176
  5.7 0.0 copy-start.5
  5.7 0.7 %copy-done.5 = f32[4096]{0:T(1024)S(1)} copy-done((f32[4096]{0:T(1024)S(1)}, f32[4096]{0:T(1024)}, u32[]{:S(2)}) %copy-start.5) | copy-done | bytes 16408
  6.4 4.3 %deposit.1 = (f32[6,4096]{1,0:T(8,128)}, f32[1296,128]{1,0:T(8,128)S(1)}, f32[1296,128]{1,0:T(8,128)S(1)}, f32[704,128]{1,0:T(8,128)S(1)}) custom-call(s32[32]{0:T(128)S(1)} %copy-done.6, s32[32]{0:T(128)S(1)} %copy-done.7, f32[3,4096]{1,0:T(4,128)S(1)} %copy-done.2, s32[3,4096]{1,0:T(4,128)S(1)} %copy-done.3, f32[3,4096]{1,0:T(4,128)S(1)} %copy-done.4, ...), custom_call_target="tpu_custom_call" | custom-call | tf_op jit(solution)/shard_map/deposit/pallas_call | solution.py:664
  10.7 27.2 %exchange.1 = (f32[1296,128]{1,0:T(8,128)S(1)}, f32[1296,128]{1,0:T(8,128)S(1)}) custom-call(f32[1296,128]{1,0:T(8,128)S(1)} %get-tuple-element.13.mom_in, f32[1296,128]{1,0:T(8,128)S(1)} %get-tuple-element.14.mass_in), custom_call_target="tpu_custom_call" | custom-call | tf_op jit(solution)/shard_map/exchange/pallas_call | solution.py:691
  37.9 5.1 %collect.1 = (f32[3,4096]{1,0:T(4,128)}, f32[9,4096]{1,0:T(8,128)}, f32[3,16,32,64]{3,2,1,0:T(8,128)}) custom-call(s32[32]{0:T(128)S(1)} %copy-done.6, f32[1296,128]{1,0:T(8,128)S(1)} %get-tuple-element.15.mom_ref, f32[1296,128]{1,0:T(8,128)S(1)} %get-tuple-element.16.mass_ref, f32[704,128]{1,0:T(8,128)S(1)} %get-tuple-element.17.shared_ref), custom_call_target="tpu_custom_call" | custom-call | tf_op jit(solution)/shard_map/collect/pallas_call | solution.py:714
Async XLA Ops:
  0.6 0.7 %copy-start.6 = (s32[32]{0:T(128)S(1)}, s32[32]{0:T(128)}, u32[]{:S(2)}) copy-start(s32[32]{0:T(128)} %tile_ref.3) | copy-start | bytes 388
  0.6 0.7 %copy-start.7 = (s32[32]{0:T(128)S(1)}, s32[32]{0:T(128)}, u32[]{:S(2)}) copy-start(s32[32]{0:T(128)} %count_ref.1) | copy-start | bytes 388
  1.3 0.9 %copy-start = (f32[9,4096]{1,0:T(8,128)S(1)}, f32[9,4096]{1,0:T(8,128)}, u32[]{:S(2)}) copy-start(f32[9,4096]{1,0:T(8,128)} %affine_ref.1) | copy-start | bytes 442372
  2.3 0.9 %copy-start.1 = (f32[6,4096]{1,0:T(8,128)S(1)}, f32[6,4096]{1,0:T(8,128)}, u32[]{:S(2)}) copy-start(f32[6,4096]{1,0:T(8,128)} %stress_ref.1) | copy-start | bytes 294916
  3.2 0.8 %copy-start.2 = (f32[3,4096]{1,0:T(4,128)S(1)}, f32[3,4096]{1,0:T(4,128)}, u32[]{:S(2)}) copy-start(f32[3,4096]{1,0:T(4,128)} %frac_ref.1) | copy-start | bytes 147460
  4.0 0.8 %copy-start.3 = (s32[3,4096]{1,0:T(4,128)S(1)}, s32[3,4096]{1,0:T(4,128)}, u32[]{:S(2)}) copy-start(s32[3,4096]{1,0:T(4,128)} %offset_ref.1) | copy-start | bytes 147460
  4.8 0.8 %copy-start.4 = (f32[3,4096]{1,0:T(4,128)S(1)}, f32[3,4096]{1,0:T(4,128)}, u32[]{:S(2)}) copy-start(f32[3,4096]{1,0:T(4,128)} %velocity_ref.1) | copy-start | bytes 147460
  5.7 0.7 %copy-start.5 = (f32[4096]{0:T(1024)S(1)}, f32[4096]{0:T(1024)}, u32[]{:S(2)}) copy-start(f32[4096]{0:T(1024)} %param.13) | copy-start | bytes 49156

commit v2 on v1

--- a/solution.py
+++ b/solution.py
@@ -119,6 +119,18 @@
 
 
 def deposit_kernel(
+    tile_hbm,
+    count_hbm,
+    frac_hbm,
+    offset_hbm,
+    velocity_hbm,
+    affine_hbm,
+    stress_hbm,
+    mass_hbm,
+    mom,
+    mass,
+    shared_ref,
+    stress_out,
     tile_ref,
     count_ref,
     frac_ref,
@@ -127,17 +139,62 @@
     affine_ref,
     stress_ref,
     mass_ref,
-    new_stress_ref,
-    mom_ref,
-    grid_mass_ref,
-    shared_ref,
     gathered,
     table,
-    stress_out,
+    placed_high,
+    placed_low,
+    z_send,
+    z_recv,
+    x_send,
+    x_recv,
+    y_send,
+    y_recv,
+    load_sem,
+    send_sem,
+    recv_sem,
 ):
+    axes = ("gx", "gy", "gz")
+
+    def device(dx, dy, dz):
+        place = []
+        for axis, step in zip(axes, (dx, dy, dz)):
+            size = lax.axis_size(axis)
+            moved = lax.axis_index(axis)
+            if step:
+                moved = moved + step
+                moved = jnp.where(moved < 0, size - 1, jnp.where(moved >= size, 0, moved))
+            place.append(moved)
+        return tuple(place)
+
+    z_sides = [device(0, 0, -1), device(0, 0, 1)]
+    x_sides = [device(-1, 0, 0), device(1, 0, 0)]
+    y_sides = [device(0, -1, 0), device(0, 1, 0)]
+    barrier = pltpu.get_barrier_semaphore()
+    for target in z_sides + x_sides + y_sides:
+        pl.semaphore_signal(barrier, inc=1, device_id=target, device_id_type=MESH)
+    loads = [
+        pltpu.make_async_copy(source, target, load_sem.at[index])
+        for index, (source, target) in enumerate(
+            (
+                (frac_hbm, frac_ref),
+                (offset_hbm, offset_ref),
+                (velocity_hbm, velocity_ref),
+                (affine_hbm, affine_ref),
+                (stress_hbm, stress_ref),
+                (mass_hbm, mass_ref),
+                (count_hbm, count_ref),
+                (tile_hbm, tile_ref),
+            )
+        )
+    ]
+    for load in loads:
+        load.start()
+
     blocks = mass_ref.shape[0]
-    lane = lax.broadcasted_iota(jnp.int32, (1, LANES), 1)
+    lane_row = lax.broadcasted_iota(jnp.int32, (1, LANES), 1)
     stride = 48
+    for load in loads:
+        load.wait()
     for block in range(blocks):
         cols = slice(block * BLOCK, (block + 1) * BLOCK)
         at = block * stride
@@ -146,22 +203,26 @@
         gathered[at + 16 : at + 19, :] = velocity_ref[:, cols]
         gathered[at + 24 : at + 33, :] = affine_ref[:, cols]
         gathered[at + 40 : at + 46, :] = stress_ref[:, cols]
-        row = T_MASS * blocks + block
+        row = (T_MASS - T_SHARED) * blocks + block
         table[row : row + 1, :] = jnp.where(
-            lane < count_ref[block], mass_ref[block : block + 1, :], 0.0
+            lane_row < count_ref[block], mass_ref[block : block + 1, :], 0.0
         )
 
     def dense(component):
         return gathered[pl.ds(component, blocks, stride=stride), :]
 
     def put(index, value):
-        table[index * blocks : (index + 1) * blocks, :] = value
+        if index < T_SHARED:
+            shared_ref[index * blocks : (index + 1) * blocks, :] = value
+        else:
+            start = (index - T_SHARED) * blocks
+            table[start : start + blocks, :] = value
 
     affine = [dense(24 + component) for component in range(9)]
     stress = stress_update([dense(40 + component) for component in range(6)], affine)
     for component in range(6):
         stress_out[component * blocks : (component + 1) * blocks, :] = stress[component]
-    live_mass = table[T_MASS * blocks : (T_MASS + 1) * blocks, :]
+    live_mass = table[(T_MASS - T_SHARED) * blocks : (T_MASS - T_SHARED + 1) * blocks, :]
     for row_dim in range(3):
         put(T_MV + row_dim, live_mass * dense(16 + row_dim))
         for col_dim in range(3):
@@ -198,13 +259,6 @@
     for index in range(5):
         put(T_LY + index, spline[1][index])
         put(T_LZ + index, spline[2][index])
-    shared_ref[...] = table[: T_SHARED * blocks, :]
-    for block in range(blocks):
-        new_stress_ref[:, block * BLOCK : (block + 1) * BLOCK] = stress_out[
-            pl.ds(block, 6, stride=blocks), :
-        ]
-    mom_ref[...] = jnp.zeros_like(mom_ref)
-    grid_mass_ref[...] = jnp.zeros_like(grid_mass_ref)
 
     lanes = lax.broadcasted_iota(jnp.int32, (8, 32), 1)
     channel = [(lanes >= 8 * index) & (lanes < 8 * index + 8) for index in range(4)]
@@ -213,7 +267,11 @@
 
     def block_sums(block):
         def row(index):
-            return jnp.broadcast_to(table[pl.ds(index * blocks + block, 1), :], (8, LANES))
+            if index < T_SHARED:
+                value = shared_ref[pl.ds(index * blocks + block, 1), :]
+            else:
+                value = table[pl.ds((index - T_SHARED) * blocks + block, 1), :]
+            return jnp.broadcast_to(value, (8, LANES))
 
         wy, wyd = axis_weights(row, T_LY, T_MY, T_RY, T_OY, T_Y)
         wz, wzd = axis_weights(row, T_LZ, T_MZ, T_RZ, T_OZ, T_Z)
@@ -249,87 +307,80 @@
             + product(left_low, right_high)
         )
 
-    def scatter(block, sums):
-        tile_x, tile_y, tile_z = tile_coords(tile_ref, block)
-        starts = (0, PITCH - 8, 2 * PITCH - 16, LANES - 24)
-        places, moved = [], []
+    starts = (0, PITCH - 8, 2 * PITCH - 16, LANES - 24)
+
+    def group_place(step, sums):
+        rows = pl.ds(pl.multiple_of(step * 8 * GROUP, 8 * GROUP), 8 * GROUP)
+        heights = [4 * (tile_ref[step * GROUP + member] & 7) for member in range(GROUP)]
         for node in range(6):
-            part = sums[8 * node : 8 * node + 8]
-            places.append(pl.ds(pl.multiple_of((4 * tile_x + node) * PY + 4 * tile_y, 4), 8))
-            moved.append(
-                [
+            mom_rows, mass_rows = [], []
+            for member in range(GROUP):
+                part = sums[member][8 * node : 8 * node + 8]
+                moved = [
                     pltpu.roll(
                         jnp.concatenate([jnp.where(channel[index], part, 0.0), rest], axis=1),
-                        starts[index] + 4 * tile_z,
+                        starts[index] + heights[member],
                         axis=1,
                     )
                     for index in range(4)
                 ]
-            )
-        mom = [mom_ref[at, :] for at in places]
-        mass = [grid_mass_ref[at, :] for at in places]
-        for node, at in enumerate(places):
-            mom_ref[at, :] = mom[node] + moved[node][0] + moved[node][1] + moved[node][2]
-            grid_mass_ref[at, :] = mass[node] + moved[node][3]
+                mom_rows.append(moved[0] + moved[1] + moved[2])
+                mass_rows.append(moved[3])
+            for column, values in enumerate((mom_rows, mass_rows)):
+                high, low = split(jnp.concatenate(values, axis=0))
+                cols = slice(column * LANES, (column + 1) * LANES)
+                placed_high[node, rows, cols] = high
+                placed_low[node, rows, cols] = low
 
     def group_sums(step):
         return tuple(block_sums(step * GROUP + member) for member in range(GROUP))
 
-    def group_scatter(step, sums):
-        for member in range(GROUP):
-            scatter(step * GROUP + member, sums[member])
-
     def group(step, sums):
         following = group_sums(step)
-        group_scatter(step - 1, sums)
+        group_place(step - 1, sums)
         return following
 
     steps = blocks // GROUP
-    group_scatter(steps - 1, lax.fori_loop(1, steps, group, group_sums(0)))
-
-
-def exchange_kernel(
-    mom_in,
-    mass_in,
-    mom,
-    mass,
-    z_send,
-    z_recv,
-    xm_recv,
-    xs_send,
-    xs_recv,
-    y_send,
-    y_recv,
-    e_send,
-    e_recv,
-    send_sem,
-    recv_sem,
-):
-    axes = ("gx", "gy", "gz")
-    me = {axis: lax.axis_index(axis) for axis in axes}
-    count = {axis: lax.axis_size(axis) for axis in axes}
-
-    def device(dx, dy, dz):
-        return tuple(
-            lax.rem(me[axis] + count[axis] + step, count[axis])
-            for axis, step in zip(axes, (dx, dy, dz))
-        )
-
-    z_steps = [(0, 0, -1), (0, 0, 1)]
-    x_steps = [(-1, 0, 0), (1, 0, 0)]
-    y_steps = [(0, -1, 0), (0, 1, 0)]
-    e_steps = [(-1, -1, 0), (-1, 1, 0), (1, -1, 0), (1, 1, 0)]
-    barrier = pltpu.get_barrier_semaphore()
-    for step in z_steps + x_steps + y_steps + e_steps:
-        pl.semaphore_signal(barrier, inc=1, device_id=device(*step), device_id_type=MESH)
-
-    def copy(src, dst, slot, step):
+    group_place(steps - 1, lax.fori_loop(1, steps, group, group_sums(0)))
+
+    spots = 8 * blocks
+    spot = lax.broadcasted_iota(jnp.int32, (8, spots), 1)
+    owner = spot >> 3
+    tiles = jnp.zeros((8, spots), jnp.int32)
+    for block in range(blocks):
+        tiles = jnp.where(owner == block, tile_ref[block], tiles)
+    target = ((tiles >> 7) << 10) + (((tiles >> 3) & 15) << 2) + (spot & 7)
+    y_row = lax.broadcasted_iota(jnp.int32, (8, spots), 0)
+    chooser = jnp.concatenate(
+        [
+            jnp.where(target == y_row + (1024 * tile_x + start), 1.0, 0.0)
+            for tile_x in range(CX // 4)
+            for start in range(0, PY, 8)
+        ],
+        axis=0,
+    ).astype(jnp.bfloat16)
+    for node in range(6):
+        layers = jnp.dot(
+            chooser, placed_high[node], preferred_element_type=jnp.float32
+        ) + jnp.dot(chooser, placed_low[node], preferred_element_type=jnp.float32)
+        for tile_x in range(CX // 4):
+            part = layers[tile_x * PY : (tile_x + 1) * PY]
+            x = 4 * tile_x + node
+            at = slice(x * PY, (x + 1) * PY)
+            if node < 4 or x >= CX:
+                mom[at, :] = part[:, :LANES]
+                mass[at, :] = part[:, LANES:]
+            else:
+                mom[at, :] += part[:, :LANES]
+                mass[at, :] += part[:, LANES:]
+
+    def copy(src, dst, slot, target):
         return pltpu.make_async_remote_copy(
             src_ref=src,
             dst_ref=dst,
             send_sem=send_sem.at[slot],
             recv_sem=recv_sem.at[slot],
-            device_id=device(*step),
+            device_id=target,
             device_id_type=MESH,
         )
 
@@ -338,46 +389,37 @@
     in_pitch = lax.rem(lane, PITCH)
     third = PY // 3
     lane3 = lane[:third]
-    in_pitch3 = in_pitch[:third]
-    in_mom3 = in_mom[:third]
-
-    for side in range(2):
-        shift = 0 if side == 0 else LANES - CZ
-
-        def pack(x, carry):
-            packed, packed_mass = carry
+
+    def pack(step, carry):
+        packed, packed_mass = list(carry[:2]), list(carry[2:])
+        for member in range(3):
+            x = 3 * step + member
             at = pl.ds(pl.multiple_of(x * PY, 8), PY)
             mine = (in_pitch >= 2 * x) & (in_pitch < 2 * x + 2) & in_mom
-            packed = jnp.where(
-                mine, pltpu.roll(mom_in[at, :], lax.rem(2 * x + shift, LANES), axis=1), packed
-            )
-            layer = mass_in[at, :]
-            for group in range(3):
-                start = PITCH * group
-                here = (lane3 >= start + 2 * x) & (lane3 < start + 2 * x + 2)
-                packed_mass = jnp.where(
-                    here,
-                    pltpu.roll(
-                        layer[group * third : (group + 1) * third],
-                        lax.rem(start + 2 * x + shift, LANES),
-                        axis=1,
-                    ),
-                    packed_mass,
+            for side, shift in enumerate((0, LANES - CZ)):
+                packed[side] = jnp.where(
+                    mine, pltpu.roll(mom[at, :], 2 * x + shift, axis=1), packed[side]
                 )
-            return packed, packed_mass
-
-        packed, packed_mass = lax.fori_loop(
-            0,
-            PX,
-            pack,
-            (jnp.zeros((PY, LANES), jnp.float32), jnp.zeros((third, LANES), jnp.float32)),
-        )
-        z_send[side, :PY, :] = packed
-        z_send[side, PY:, :] = packed_mass
-
-    pl.semaphore_wait(barrier, 10)
+                for part in range(3):
+                    start = PITCH * part
+                    rows = pl.ds(pl.multiple_of(x * PY + part * third, 8), third)
+                    here = (lane3 >= start + 2 * x) & (lane3 < start + 2 * x + 2)
+                    packed_mass[side] = jnp.where(
+                        here,
+                        pltpu.roll(mass[rows, :], start + 2 * x + shift, axis=1),
+                        packed_mass[side],
+                    )
+        return tuple(packed + packed_mass)
+
+    empty = jnp.zeros((PY, LANES), jnp.float32)
+    packed = lax.fori_loop(0, PX // 3, pack, (empty, empty, empty[:third], empty[:third]))
+    for side in range(2):
+        z_send[side, :PY, :] = packed[side]
+        z_send[side, PY:, :] = packed[2 + side]
+
+    pl.semaphore_wait(barrier, 6)
     z_copies = [
-        copy(z_send.at[side], z_recv.at[1 - side], side, z_steps[side]) for side in range(2)
+        copy(z_send.at[side], z_recv.at[1 - side], side, z_sides[side]) for side in range(2)
     ]
     for c in z_copies:
         c.start()
@@ -389,110 +431,103 @@
     low3 = lane3 < 2
     high3 = (lane3 >= CZ) & (lane3 < CZ + 2)
 
-    def unpack(x, carry):
-        at = pl.ds(pl.multiple_of(x * PY, 8), PY)
-        from_low = pltpu.roll(z_recv[0, :PY, :], lax.rem(LANES - 2 * x, LANES), axis=1)
-        from_high = pltpu.roll(z_recv[1, :PY, :], lax.rem(LANES + CZ - 2 * x, LANES), axis=1)
-        mom[at, :] = (
-            mom_in[at, :] + jnp.where(low, from_low, 0.0) + jnp.where(high, from_high, 0.0)
-        )
-        for group in range(3):
-            start = PITCH * group
-            rows = pl.ds(pl.multiple_of(x * PY + group * third, 8), third)
-            from_low = pltpu.roll(
-                z_recv[0, PY:, :], lax.rem(2 * LANES - start - 2 * x, LANES), axis=1
-            )
-            from_high = pltpu.roll(
-                z_recv[1, PY:, :], lax.rem(2 * LANES + CZ - start - 2 * x, LANES), axis=1
-            )
-            mass[rows, :] = (
-                mass_in[rows, :]
-                + jnp.where(low3, from_low, 0.0)
-                + jnp.where(high3, from_high, 0.0)
-            )
+    def unpack(step, carry):
+        for member in range(3):
+            x = 3 * step + member
+            at = pl.ds(pl.multiple_of(x * PY, 8), PY)
+            from_low = pltpu.roll(z_recv[0, :PY, :], LANES - 2 * x, axis=1)
+            from_high = pltpu.roll(z_recv[1, :PY, :], LANES + CZ - 2 * x, axis=1)
+            mom[at, :] += jnp.where(low, from_low, jnp.where(high, from_high, 0.0))
+            for part in range(3):
+                start = PITCH * part
+                rows = pl.ds(pl.multiple_of(x * PY + part * third, 8), third)
+                from_low = pltpu.roll(z_recv[0, PY:, :], 2 * LANES - start - 2 * x, axis=1)
+                from_high = pltpu.roll(
+                    z_recv[1, PY:, :], 2 * LANES + CZ - start - 2 * x, axis=1
+                )
+                mass[rows, :] += jnp.where(low3, from_low, jnp.where(high3, from_high, 0.0))
         return carry
 
-    lax.fori_loop(0, PX, unpack, 0)
-
-    firsts = (0, CX)
+    lax.fori_loop(0, PX // 3, unpack, 0)
+
+    front = lane < 64
+    firsts = (0, CX * PY)
+    for side in range(2):
+        first = firsts[side]
+        x_send[side, : 2 * PY, :] = mom[first : first + 2 * PY, :]
+        x_send[side, 2 * PY :, :] = mass[first : first + PY, :] + pltpu.roll(
+            mass[first + PY : first + 2 * PY, :], 64, axis=1
+        )
+    x_copies = [
+        copy(x_send.at[side], x_recv.at[1 - side], 2 + side, x_sides[side]) for side in range(2)
+    ]
+    for c in x_copies:
+        c.start()
+    for c in x_copies:
+        c.wait()
+    for side in range(2):
+        first = firsts[side]
+        mom[first : first + 2 * PY, :] += x_recv[side, : 2 * PY, :]
+        got = x_recv[side, 2 * PY :, :]
+        mass[first : first + PY, :] += jnp.where(front, got, 0.0)
+        mass[first + PY : first + 2 * PY, :] += jnp.where(
+            front, pltpu.roll(got, 64, axis=1), 0.0
+        )
+
     y_firsts = (0, CY)
-    copies = []
-    for side in range(2):
-        first = firsts[side] * PY
-        xs_send[side] = mass[first : first + PY, :] + pltpu.roll(
-            mass[first + PY : first + 2 * PY, :], 64, axis=1
-        )
-        copies.append(
-            copy(
-                mom.at[pl.ds(first, 2 * PY), :], xm_recv.at[1 - side], 2 + side, x_steps[side]
-            )
-        )
-        copies.append(copy(xs_send.at[side], xs_recv.at[1 - side], 4 + side, x_steps[side]))
-    for c in copies:
-        c.start()
-    more = []
     for side in range(2):
         y0 = y_firsts[side]
         y_send[side, 0:PX, :] = mom[pl.ds(y0, PX, stride=PY), :]
-        y_send[side, 24 : 24 + PX, :] = mom[pl.ds(y0 + 1, PX, stride=PY), :]
-        y_send[side, 48 : 48 + PX, :] = mass[pl.ds(y0, PX, stride=PY), :] + pltpu.roll(
+        y_send[side, PX : 2 * PX, :] = mom[pl.ds(y0 + 1, PX, stride=PY), :]
+        y_send[side, 2 * PX : 3 * PX, :] = mass[pl.ds(y0, PX, stride=PY), :] + pltpu.roll(
             mass[pl.ds(y0 + 1, PX, stride=PY), :], 64, axis=1
         )
-        y_send[side, PX:24, :] = jnp.zeros((24 - PX, LANES), jnp.float32)
-        y_send[side, 24 + PX : 48, :] = jnp.zeros((24 - PX, LANES), jnp.float32)
-        y_send[side, 48 + PX : 72, :] = jnp.zeros((24 - PX, LANES), jnp.float32)
-        more.append(copy(y_send.at[side], y_recv.at[1 - side], 6 + side, y_steps[side]))
-    for edge in range(4):
-        x0, y0 = firsts[edge // 2], y_firsts[edge % 2]
-        for layer in range(2):
-            at = (x0 + layer) * PY + y0
-            e_send[edge, 2 * layer : 2 * layer + 2, :] = mom[at : at + 2, :]
-            e_send[edge, 4 + 2 * layer : 6 + 2 * layer, :] = mass[at : at + 2, :]
-        more.append(copy(e_send.at[edge], e_recv.at[3 - edge], 8 + edge, e_steps[edge]))
-    for c in more:
+        y_send[side, 3 * PX :, :] = jnp.zeros((2, LANES), jnp.float32)
+    y_copies = [
+        copy(y_send.at[side], y_recv.at[1 - side], 4 + side, y_sides[side]) for side in range(2)
+    ]
+    for c in y_copies:
         c.start()
-    for c in copies + more:
+    for c in y_copies:
         c.wait()
-    front = lane < 64
-    front_x = lax.broadcasted_iota(jnp.int32, (PX, LANES), 1) < 64
-    for side in range(2):
-        first = firsts[side] * PY
-        mom[first : first + 2 * PY, :] += xm_recv[side]
-        got = xs_recv[side]
-        mass[first : first + PY, :] += jnp.where(front, got, 0.0)
-        mass[first + PY : first + 2 * PY, :] += jnp.where(
-            front, pltpu.roll(got, 64, axis=1), 0.0
-        )
     for side in range(2):
         y0 = y_firsts[side]
-        got = y_recv[side, 48 : 48 + PX, :]
+        got = y_recv[side, 2 * PX : 3 * PX, :]
         at0 = pl.ds(y0, PX, stride=PY)
         at1 = pl.ds(y0 + 1, PX, stride=PY)
         mom[at0, :] = mom[at0, :] + y_recv[side, 0:PX, :]
-        mom[at1, :] = mom[at1, :] + y_recv[side, 24 : 24 + PX, :]
-        mass[at0, :] = mass[at0, :] + jnp.where(front_x, got, 0.0)
-        mass[at1, :] = mass[at1, :] + jnp.where(front_x, pltpu.roll(got, 64, axis=1), 0.0)
-    for edge in range(4):
-        x0, y0 = firsts[edge // 2], y_firsts[edge % 2]
-        for layer in range(2):
-            at = (x0 + layer) * PY + y0
-            mom[at : at + 2, :] += e_recv[edge, 2 * layer : 2 * layer + 2, :]
-            mass[at : at + 2, :] += e_recv[edge, 4 + 2 * layer : 6 + 2 * layer, :]
+        mom[at1, :] = mom[at1, :] + y_recv[side, PX : 2 * PX, :]
+        mass[at0, :] = mass[at0, :] + jnp.where(front[:PX], got, 0.0)
+        mass[at1, :] = mass[at1, :] + jnp.where(front[:PX], pltpu.roll(got, 64, axis=1), 0.0)
 
 
 def collect_kernel(
-    tile_ref,
+    tile_hbm,
     mom_ref,
     mass_ref,
     shared_ref,
+    stress_in,
     new_velocity_ref,
     new_affine_ref,
+    new_stress_hbm,
+    grid_velocity_hbm,
+    tile_ref,
+    new_stress_ref,
     grid_velocity_ref,
     velocity,
     partial,
     final,
+    copy_sem,
 ):
-    blocks = tile_ref.shape[0]
+    blocks = tile_hbm.shape[0]
+    tile_copy = pltpu.make_async_copy(tile_hbm, tile_ref, copy_sem.at[0])
+    tile_copy.start()
+    for block in range(blocks):
+        new_stress_ref[:, block * BLOCK : (block + 1) * BLOCK] = stress_in[
+            pl.ds(block, 6, stride=blocks), :
+        ]
+    stress_copy = pltpu.make_async_copy(new_stress_ref, new_stress_hbm, copy_sem.at[1])
+    stress_copy.start()
     width_x = lax.axis_size("gx") * CX
     height_y = lax.axis_size("gy") * CY
     depth_z = lax.axis_size("gz") * CZ
@@ -546,6 +581,9 @@
         return carry
 
     lax.fori_loop(0, CX // 4, output, 0)
+    grid_copy = pltpu.make_async_copy(grid_velocity_ref, grid_velocity_hbm, copy_sem.at[2])
+    grid_copy.start()
+    tile_copy.wait()
 
     lanes = lax.broadcasted_iota(jnp.int32, (8, LANES), 1)
 
@@ -643,6 +681,8 @@
         cols = slice(block * BLOCK, (block + 1) * BLOCK)
         new_velocity_ref[:, cols] = final[pl.ds(block, 3, stride=blocks), :]
         new_affine_ref[:, cols] = final[pl.ds(3 * blocks + block, 9, stride=blocks), :]
+    stress_copy.wait()
+    grid_copy.wait()
 
 
 def shards(
@@ -658,76 +698,83 @@
     blocks = block_tile.shape[0]
     points = blocks * BLOCK
     vmem = pl.BlockSpec(memory_space=pltpu.VMEM)
-    smem = pl.BlockSpec(memory_space=pltpu.SMEM)
+    hbm = pl.BlockSpec(memory_space=pltpu.HBM)
     f32 = jnp.float32
     grid_shape = jax.ShapeDtypeStruct((ROWS, LANES), f32)
-    new_stress, mom, mass, shared = pl.pallas_call(
+    face = PY + PY // 3
+    arguments = [
+        pltpu.with_memory_space_constraint(value, pltpu.HBM)
+        for value in (
+            block_tile,
+            block_count,
+            point_frac,
+            cell_offset,
+            point_velocity,
+            point_affine,
+            point_stress,
+            point_mass.reshape(blocks, BLOCK),
+        )
+    ]
+    mom, mass, shared, stress = pl.pallas_call(
         deposit_kernel,
         name="deposit",
         out_shape=(
-            jax.ShapeDtypeStruct((6, points), f32),
             grid_shape,
             grid_shape,
             jax.ShapeDtypeStruct((T_SHARED * blocks, LANES), f32),
+            jax.ShapeDtypeStruct((6 * blocks, LANES), f32),
         ),
-        in_specs=[smem, smem] + [vmem] * 6,
+        in_specs=[hbm] * 8,
         out_specs=(vmem,) * 4,
         scratch_shapes=[
+            pltpu.SMEM((blocks,), jnp.int32),
+            pltpu.SMEM((blocks,), jnp.int32),
+            pltpu.VMEM((3, points), f32),
+            pltpu.VMEM((3, points), jnp.int32),
+            pltpu.VMEM((3, points), f32),
+            pltpu.VMEM((9, points), f32),
+            pltpu.VMEM((6, points), f32),
+            pltpu.VMEM((blocks, BLOCK), f32),
             pltpu.VMEM((48 * blocks, LANES), f32),
-            pltpu.VMEM((T_ALL * blocks, LANES), f32),
-            pltpu.VMEM((8 * blocks, LANES), f32),
-        ],
-        compiler_params=pltpu.CompilerParams(vmem_limit_bytes=VMEM_LIMIT),
-    )(
-        block_tile,
-        block_count,
-        point_frac,
-        cell_offset,
-        point_velocity,
-        point_affine,
-        point_stress,
-        point_mass.reshape(blocks, BLOCK),
-    )
-    mom, mass = pl.pallas_call(
-        exchange_kernel,
-        name="exchange",
-        out_shape=(grid_shape, grid_shape),
-        in_specs=[vmem] * 2,
-        out_specs=(vmem,) * 2,
-        scratch_shapes=[
-            pltpu.VMEM((2, PY + PY // 3, LANES), f32),
-            pltpu.VMEM((2, PY + PY // 3, LANES), f32),
-            pltpu.VMEM((2, 2 * PY, LANES), f32),
-            pltpu.VMEM((2, PY, LANES), f32),
-            pltpu.VMEM((2, PY, LANES), f32),
-            pltpu.VMEM((2, 72, LANES), f32),
-            pltpu.VMEM((2, 72, LANES), f32),
-            pltpu.VMEM((4, 8, LANES), f32),
-            pltpu.VMEM((4, 8, LANES), f32),
-            pltpu.SemaphoreType.DMA((12,)),
-            pltpu.SemaphoreType.DMA((12,)),
+            pltpu.VMEM(((T_ALL - T_SHARED) * blocks, LANES), f32),
+            pltpu.VMEM((6, 8 * blocks, 2 * LANES), jnp.bfloat16),
+            pltpu.VMEM((6, 8 * blocks, 2 * LANES), jnp.bfloat16),
+            pltpu.VMEM((2, face, LANES), f32),
+            pltpu.VMEM((2, face, LANES), f32),
+            pltpu.VMEM((2, 3 * PY, LANES), f32),
+            pltpu.VMEM((2, 3 * PY, LANES), f32),
+            pltpu.VMEM((2, 3 * PX + 2, LANES), f32),
+            pltpu.VMEM((2, 3 * PX + 2, LANES), f32),
+            pltpu.SemaphoreType.DMA((8,)),
+            pltpu.SemaphoreType.DMA((6,)),
+            pltpu.SemaphoreType.DMA((6,)),
         ],
         compiler_params=pltpu.CompilerParams(
             collective_id=0, has_side_effects=True, vmem_limit_bytes=VMEM_LIMIT
         ),
-    )(mom, mass)
-    new_velocity, new_affine, grid_velocity = pl.pallas_call(
+    )(*arguments)
+    new_velocity, new_affine, new_stress, grid_velocity = pl.pallas_call(
         collect_kernel,
         name="collect",
         out_shape=(
             jax.ShapeDtypeStruct((3, points), f32),
             jax.ShapeDtypeStruct((9, points), f32),
+            jax.ShapeDtypeStruct((6, points), f32),
             jax.ShapeDtypeStruct((3, CX, CZ, CY), f32),
         ),
-        in_specs=[smem] + [vmem] * 3,
-        out_specs=(vmem,) * 3,
+        in_specs=[hbm] + [vmem] * 4,
+        out_specs=(vmem, vmem, hbm, hbm),
         scratch_shapes=[
+            pltpu.SMEM((blocks,), jnp.int32),
+            pltpu.VMEM((6, points), f32),
+            pltpu.VMEM((3, CX, CZ, CY), f32),
             pltpu.VMEM((ROWS, LANES), f32),
             pltpu.VMEM((12 * 8 * blocks, LANES), f32),
             pltpu.VMEM((12 * blocks, LANES), f32),
+            pltpu.SemaphoreType.DMA((3,)),
         ],
         compiler_params=pltpu.CompilerParams(vmem_limit_bytes=VMEM_LIMIT),
-    )(block_tile, mom, mass, shared)
+    )(arguments[0], mom, mass, shared, stress)
     return (new_velocity, new_affine, new_stress, jnp.swapaxes(grid_velocity, 2, 3))
 
 

time: 43.4 us -> 36.6 us (0.84)
  local copies, waits for them, and re-layouts: 5.74 us -> 0 us
  Pallas kernels: 36.6 us -> 35.8 us
    unnamed x16 -> x0, local copies, waits for them, and re-layouts: 5.74 us -> none
    pallas_call x1, Pallas kernels: 5.15 us -> 4.52 us  [shards(): pl.pallas_call(collect_kernel, name='collect', out_shape=(jax.ShapeDtypeS...]
    pallas_call x2 -> x1, Pallas kernels: 31.5 us -> 31.3 us  [shards(): pl.pallas_call(deposit_kernel, name='deposit', out_shape=(grid_shape, gri...]
where the time goes in v2:
time: 36.6 us; the launch traced here: 36.4 us
  Pallas kernels  35.8 us (98%)
  between operations  0.64 us (2%)
    pallas_call x1, Pallas kernels, shards(): pl.pallas_call(deposit_kernel, name='deposit', out_shape=(grid_shape, gri...  31.3 us
    pallas_call x1, Pallas kernels, shards(): pl.pallas_call(collect_kernel, name='collect', out_shape=(jax.ShapeDtypeS...  4.52 us

profile of v2, /device:TPU:1, one launch (start us, length us, event | category | flops | bytes accessed | tf_op | source)
XLA Modules:
  0.0 36.4 jit_solution(15169146703530693498)
XLA Ops:
  0.6 31.3 %deposit.1 = (f32[1296,128]{1,0:T(8,128)S(1)}, f32[1296,128]{1,0:T(8,128)S(1)}, f32[704,128]{1,0:T(8,128)S(1)}, f32[192,128]{1,0:T(8,128)S(1)}) custom-call(s32[32]{0:T(128)} %tile_hbm.3, s32[32]{0:T(128)} %count_hbm.1, f32[3,4096]{1,0:T(4,128)} %frac_hbm.1, s32[3,4096]{1,0:T(4,128)} %offset_hbm.1, f32[3,4096]{1,0:T(4,128)} %velocity_hbm.1, ...), custom_call_target="tpu_custom_call" | custom-call | tf_op jit(solution)/shard_map/deposit/pallas_call | solution.py:718
  31.9 4.5 %collect.1 = (f32[3,4096]{1,0:T(4,128)}, f32[9,4096]{1,0:T(8,128)}, f32[6,4096]{1,0:T(8,128)}, f32[3,16,32,64]{3,2,1,0:T(8,128)}) custom-call(s32[32]{0:T(128)} %tile_hbm.3, f32[1296,128]{1,0:T(8,128)S(1)} %get-tuple-element.12.mom_ref, f32[1296,128]{1,0:T(8,128)S(1)} %get-tuple-element.13.mass_ref, f32[704,128]{1,0:T(8,128)S(1)} %get-tuple-element.14.shared_ref, ...), custom_call_target="tpu_custom_call" | custom-call | tf_op jit(solution)/shard_map/collect/pallas_call | solution.py:756

commit v3 on v2

--- a/solution.py
+++ b/solution.py
@@ -32,6 +32,7 @@
 LANES = 128
 ROWS = PX * PY
 GROUP = 4
+UNROLL = 6
 VMEM_LIMIT = 16 * 1024 * 1024
 MESH = pl.DeviceIdType.MESH
 
@@ -147,6 +148,8 @@
     z_recv,
     x_send,
     x_recv,
+    xz_send,
+    xz_recv,
     y_send,
     y_recv,
     load_sem,
@@ -169,8 +172,9 @@
     z_sides = [device(0, 0, -1), device(0, 0, 1)]
     x_sides = [device(-1, 0, 0), device(1, 0, 0)]
     y_sides = [device(0, -1, 0), device(0, 1, 0)]
+    xz_sides = [device(dx, 0, dz) for dx in (-1, 1) for dz in (-1, 1)]
     barrier = pltpu.get_barrier_semaphore()
-    for target in z_sides + x_sides + y_sides:
+    for target in x_sides + z_sides + xz_sides + y_sides:
         pl.semaphore_signal(barrier, inc=1, device_id=target, device_id_type=MESH)
     loads = [
         pltpu.make_async_copy(source, target, load_sem.at[index])
@@ -389,11 +393,30 @@
     in_pitch = lax.rem(lane, PITCH)
     third = PY // 3
     lane3 = lane[:third]
+    pl.semaphore_wait(barrier, 10)
+
+    firsts = (0, CX * PY)
+    for side in range(2):
+        first = firsts[side]
+        x_send[side, : 2 * PY, :] = mom[first : first + 2 * PY, :]
+        for layer in range(2):
+            start = first + layer * PY
+            at = 2 * PY + layer * third
+            x_send[side, at : at + third, :] = (
+                mass[start : start + third, :]
+                + pltpu.roll(mass[start + third : start + 2 * third, :], PITCH, axis=1)
+                + pltpu.roll(mass[start + 2 * third : start + 3 * third, :], 2 * PITCH, axis=1)
+            )
+    x_copies = [
+        copy(x_send.at[side], x_recv.at[1 - side], 2 + side, x_sides[side]) for side in range(2)
+    ]
+    for c in x_copies:
+        c.start()
 
     def pack(step, carry):
         packed, packed_mass = list(carry[:2]), list(carry[2:])
-        for member in range(3):
-            x = 3 * step + member
+        for member in range(UNROLL):
+            x = UNROLL * step + member
             at = pl.ds(pl.multiple_of(x * PY, 8), PY)
             mine = (in_pitch >= 2 * x) & (in_pitch < 2 * x + 2) & in_mom
             for side, shift in enumerate((0, LANES - CZ)):
@@ -412,28 +435,55 @@
         return tuple(packed + packed_mass)
 
     empty = jnp.zeros((PY, LANES), jnp.float32)
-    packed = lax.fori_loop(0, PX // 3, pack, (empty, empty, empty[:third], empty[:third]))
+    packed = lax.fori_loop(0, PX // UNROLL, pack, (empty, empty, empty[:third], empty[:third]))
     for side in range(2):
         z_send[side, :PY, :] = packed[side]
         z_send[side, PY:, :] = packed[2 + side]
-
-    pl.semaphore_wait(barrier, 6)
     z_copies = [
         copy(z_send.at[side], z_recv.at[1 - side], side, z_sides[side]) for side in range(2)
     ]
     for c in z_copies:
         c.start()
+
+    quad = lax.broadcasted_iota(jnp.int32, (8, LANES), 1) >> 2
+    for edge in range(4):
+        x0, z_side = CX * (edge // 2), edge % 2
+        result = [None, None]
+        for tile in range(PY // 8):
+            half, start = tile // 8, 16 * (tile % 8)
+            rows = z_send[z_side, 8 * tile : 8 * tile + 8, :]
+            mass_at = PY + 8 * (tile % 3)
+            mass_rows = z_send[z_side, mass_at : mass_at + 8, :]
+            for index in range(4):
+                if index < 3:
+                    source, at = rows, PITCH * index + 2 * x0
+                else:
+                    source, at = mass_rows, PITCH * (tile // 3) + 2 * x0
+                to = start + 4 * index
+                moved = pltpu.roll(source, (LANES + to - at) % LANES, axis=1)
+                if result[half] is None:
+                    result[half] = moved
+                else:
+                    result[half] = jnp.where(quad == to // 4, moved, result[half])
+        xz_send[edge, :8, :] = result[0]
+        xz_send[edge, 8:, :] = result[1]
+    xz_copies = [
+        copy(xz_send.at[edge], xz_recv.at[3 - edge], 6 + edge, xz_sides[edge])
+        for edge in range(4)
+    ]
+    for c in xz_copies:
+        c.start()
+
     for c in z_copies:
         c.wait()
-
     low = (in_pitch < 2) & in_mom
     high = (in_pitch >= CZ) & (in_pitch < CZ + 2) & in_mom
     low3 = lane3 < 2
     high3 = (lane3 >= CZ) & (lane3 < CZ + 2)
 
     def unpack(step, carry):
-        for member in range(3):
-            x = 3 * step + member
+        for member in range(UNROLL):
+            x = UNROLL * step + member
             at = pl.ds(pl.multiple_of(x * PY, 8), PY)
             from_low = pltpu.roll(z_recv[0, :PY, :], LANES - 2 * x, axis=1)
             from_high = pltpu.roll(z_recv[1, :PY, :], LANES + CZ - 2 * x, axis=1)
@@ -448,31 +498,45 @@
                 mass[rows, :] += jnp.where(low3, from_low, jnp.where(high3, from_high, 0.0))
         return carry
 
-    lax.fori_loop(0, PX // 3, unpack, 0)
-
-    front = lane < 64
-    firsts = (0, CX * PY)
+    lax.fori_loop(0, PX // UNROLL, unpack, 0)
+
+    for c in xz_copies:
+        c.wait()
+    lane8 = lane[:8]
     for side in range(2):
-        first = firsts[side]
-        x_send[side, : 2 * PY, :] = mom[first : first + 2 * PY, :]
-        x_send[side, 2 * PY :, :] = mass[first : first + PY, :] + pltpu.roll(
-            mass[first + PY : first + 2 * PY, :], 64, axis=1
-        )
-    x_copies = [
-        copy(x_send.at[side], x_recv.at[1 - side], 2 + side, x_sides[side]) for side in range(2)
-    ]
-    for c in x_copies:
-        c.start()
+        for layer in range(2):
+            for tile in range(PY // 8):
+                half, start = tile // 8, 16 * (tile % 8)
+                mom_value, mass_value = 0.0, 0.0
+                for z_side in range(2):
+                    source = xz_recv[2 * side + z_side, 8 * half : 8 * half + 8, :]
+                    for index in range(4):
+                        to = (PITCH * index if index < 3 else 0) + CZ * z_side
+                        at = start + 4 * index + 2 * layer
+                        moved = pltpu.roll(source, (LANES + to - at) % LANES, axis=1)
+                        here = (lane8 >= to) & (lane8 < to + 2)
+                        if index < 3:
+                            mom_value = jnp.where(here, moved, mom_value)
+                        else:
+                            mass_value = jnp.where(here, moved, mass_value)
+                at = firsts[side] + layer * PY + 8 * tile
+                mom[at : at + 8, :] += mom_value
+                mass[at : at + 8, :] += mass_value
+
     for c in x_copies:
         c.wait()
+    near3 = lane3 < PITCH
     for side in range(2):
         first = firsts[side]
         mom[first : first + 2 * PY, :] += x_recv[side, : 2 * PY, :]
-        got = x_recv[side, 2 * PY :, :]
-        mass[first : first + PY, :] += jnp.where(front, got, 0.0)
-        mass[first + PY : first + 2 * PY, :] += jnp.where(
-            front, pltpu.roll(got, 64, axis=1), 0.0
-        )
+        for layer in range(2):
+            at = 2 * PY + layer * third
+            got = x_recv[side, at : at + third, :]
+            for part in range(3):
+                start = first + layer * PY + part * third
+                moved = pltpu.roll(got, (LANES - PITCH * part) % LANES, axis=1)
+                mass[start : start + third, :] += jnp.where(near3, moved, 0.0)
+    front = lane < 64
 
     y_firsts = (0, CY)
     for side in range(2):
@@ -741,13 +805,15 @@
             pltpu.VMEM((6, 8 * blocks, 2 * LANES), jnp.bfloat16),
             pltpu.VMEM((2, face, LANES), f32),
             pltpu.VMEM((2, face, LANES), f32),
-            pltpu.VMEM((2, 3 * PY, LANES), f32),
-            pltpu.VMEM((2, 3 * PY, LANES), f32),
+            pltpu.VMEM((2, 2 * face, LANES), f32),
+            pltpu.VMEM((2, 2 * face, LANES), f32),
+            pltpu.VMEM((4, 16, LANES), f32),
+            pltpu.VMEM((4, 16, LANES), f32),
             pltpu.VMEM((2, 3 * PX + 2, LANES), f32),
             pltpu.VMEM((2, 3 * PX + 2, LANES), f32),
             pltpu.SemaphoreType.DMA((8,)),
-            pltpu.SemaphoreType.DMA((6,)),
-            pltpu.SemaphoreType.DMA((6,)),
+            pltpu.SemaphoreType.DMA((10,)),
+            pltpu.SemaphoreType.DMA((10,)),
         ],
         compiler_params=pltpu.CompilerParams(
             collective_id=0, has_side_effects=True, vmem_limit_bytes=VMEM_LIMIT

time: 36.6 us -> 33.1 us (0.904)
  Pallas kernels: 35.8 us -> 32.4 us
    pallas_call x1, Pallas kernels: 31.3 us -> 27.9 us  [shards(): pl.pallas_call(deposit_kernel, name='deposit', out_shape=(grid_shape, gri...]
where the time goes in v3:
time: 33.1 us; the launch traced here: 33 us
  Pallas kernels  32.4 us (98%)
  between operations  0.64 us (2%)
    pallas_call x1, Pallas kernels, shards(): pl.pallas_call(deposit_kernel, name='deposit', out_shape=(grid_shape, gri...  27.9 us
    pallas_call x1, Pallas kernels, shards(): pl.pallas_call(collect_kernel, name='collect', out_shape=(jax.ShapeDtypeS...  4.52 us

profile of v3, /device:TPU:1, one launch (start us, length us, event | category | flops | bytes accessed | tf_op | source)
XLA Modules:
  0.0 33.0 jit_solution(10068627095134449782)
XLA Ops:
  0.6 27.9 %deposit.1 = (f32[1296,128]{1,0:T(8,128)S(1)}, f32[1296,128]{1,0:T(8,128)S(1)}, f32[704,128]{1,0:T(8,128)S(1)}, f32[192,128]{1,0:T(8,128)S(1)}) custom-call(s32[32]{0:T(128)} %tile_hbm.3, s32[32]{0:T(128)} %count_hbm.1, f32[3,4096]{1,0:T(4,128)} %frac_hbm.1, s32[3,4096]{1,0:T(4,128)} %offset_hbm.1, f32[3,4096]{1,0:T(4,128)} %velocity_hbm.1, ...), custom_call_target="tpu_custom_call" | custom-call | tf_op jit(solution)/shard_map/deposit/pallas_call | solution.py:782
  28.5 4.5 %collect.1 = (f32[3,4096]{1,0:T(4,128)}, f32[9,4096]{1,0:T(8,128)}, f32[6,4096]{1,0:T(8,128)}, f32[3,16,32,64]{3,2,1,0:T(8,128)}) custom-call(s32[32]{0:T(128)} %tile_hbm.3, f32[1296,128]{1,0:T(8,128)S(1)} %get-tuple-element.12.mom_ref, f32[1296,128]{1,0:T(8,128)S(1)} %get-tuple-element.13.mass_ref, f32[704,128]{1,0:T(8,128)S(1)} %get-tuple-element.14.shared_ref, ...), custom_call_target="tpu_custom_call" | custom-call | tf_op jit(solution)/shard_map/collect/pallas_call | solution.py:822

commit v4 on v3

--- a/solution.py
+++ b/solution.py
@@ -32,7 +32,6 @@
 LANES = 128
 ROWS = PX * PY
 GROUP = 4
-UNROLL = 6
 VMEM_LIMIT = 16 * 1024 * 1024
 MESH = pl.DeviceIdType.MESH
 
@@ -152,6 +151,8 @@
     xz_recv,
     y_send,
     y_recv,
+    xy_send,
+    xy_recv,
     load_sem,
     send_sem,
     recv_sem,
@@ -169,13 +170,6 @@
             place.append(moved)
         return tuple(place)
 
-    z_sides = [device(0, 0, -1), device(0, 0, 1)]
-    x_sides = [device(-1, 0, 0), device(1, 0, 0)]
-    y_sides = [device(0, -1, 0), device(0, 1, 0)]
-    xz_sides = [device(dx, 0, dz) for dx in (-1, 1) for dz in (-1, 1)]
-    barrier = pltpu.get_barrier_semaphore()
-    for target in x_sides + z_sides + xz_sides + y_sides:
-        pl.semaphore_signal(barrier, inc=1, device_id=target, device_id_type=MESH)
     loads = [
         pltpu.make_async_copy(source, target, load_sem.at[index])
         for index, (source, target) in enumerate(
@@ -193,6 +187,14 @@
     ]
     for load in loads:
         load.start()
+    z_sides = [device(0, 0, -1), device(0, 0, 1)]
+    x_sides = [device(-1, 0, 0), device(1, 0, 0)]
+    y_sides = [device(0, -1, 0), device(0, 1, 0)]
+    xz_sides = [device(dx, 0, dz) for dx in (-1, 1) for dz in (-1, 1)]
+    xy_sides = [device(dx, dy, 0) for dx in (-1, 1) for dy in (-1, 1)]
+    barrier = pltpu.get_barrier_semaphore()
+    for target in z_sides + x_sides + xz_sides + y_sides + xy_sides:
+        pl.semaphore_signal(barrier, inc=1, device_id=target, device_id_type=MESH)
 
     blocks = mass_ref.shape[0]
     lane_row = lax.broadcasted_iota(jnp.int32, (1, LANES), 1)
@@ -300,15 +302,11 @@
         left_high, left_low = split(left_side)
         right_high, right_low = split(right_side)
 
-        def product(a, b):
-            return lax.dot_general(
-                a, b, (((1,), (1,)), ((), ())), preferred_element_type=jnp.float32
-            )
-
-        return (
-            product(left_high, right_high)
-            + product(left_high, right_low)
-            + product(left_low, right_high)
+        return lax.dot_general(
+            jnp.concatenate([left_high, left_high, left_low], axis=1),
+            jnp.concatenate([right_high, right_low, right_high], axis=1),
+            (((1,), (1,)), ((), ())),
+            preferred_element_type=jnp.float32,
         )
 
     starts = (0, PITCH - 8, 2 * PITCH - 16, LANES - 24)
@@ -393,7 +391,7 @@
     in_pitch = lax.rem(lane, PITCH)
     third = PY // 3
     lane3 = lane[:third]
-    pl.semaphore_wait(barrier, 10)
+    pl.semaphore_wait(barrier, 14)
 
     firsts = (0, CX * PY)
     for side in range(2):
@@ -413,32 +411,30 @@
     for c in x_copies:
         c.start()
 
-    def pack(step, carry):
-        packed, packed_mass = list(carry[:2]), list(carry[2:])
-        for member in range(UNROLL):
-            x = UNROLL * step + member
-            at = pl.ds(pl.multiple_of(x * PY, 8), PY)
-            mine = (in_pitch >= 2 * x) & (in_pitch < 2 * x + 2) & in_mom
-            for side, shift in enumerate((0, LANES - CZ)):
-                packed[side] = jnp.where(
-                    mine, pltpu.roll(mom[at, :], 2 * x + shift, axis=1), packed[side]
+    pair = jnp.where(in_mom, in_pitch >> 1, -1)
+    far = lax.rem(lane + (LANES - CZ), LANES)
+    far_pair = jnp.where(far < 3 * PITCH, lax.rem(far, PITCH) >> 1, -1)
+    pair3 = lane3 >> 1
+    far_pair3 = far[:third] >> 1
+    packed, packed_mass = [None, None], [None, None]
+    for x in range(PX):
+        at = slice(x * PY, (x + 1) * PY)
+        moved = pltpu.roll(mom[at, :], 2 * x, axis=1) if x else mom[at, :]
+        for side, which in enumerate((pair, far_pair)):
+            packed[side] = jnp.where(which == x, moved, packed[side] if x else 0.0)
+        for part in range(3):
+            start = PITCH * part
+            rows = slice(x * PY + part * third, x * PY + (part + 1) * third)
+            moved = mass[rows, :]
+            if start + 2 * x:
+                moved = pltpu.roll(moved, start + 2 * x, axis=1)
+            for side, which in enumerate((pair3, far_pair3)):
+                packed_mass[side] = jnp.where(
+                    which == start // 2 + x, moved, packed_mass[side] if start + x else 0.0
                 )
-                for part in range(3):
-                    start = PITCH * part
-                    rows = pl.ds(pl.multiple_of(x * PY + part * third, 8), third)
-                    here = (lane3 >= start + 2 * x) & (lane3 < start + 2 * x + 2)
-                    packed_mass[side] = jnp.where(
-                        here,
-                        pltpu.roll(mass[rows, :], start + 2 * x + shift, axis=1),
-                        packed_mass[side],
-                    )
-        return tuple(packed + packed_mass)
-
-    empty = jnp.zeros((PY, LANES), jnp.float32)
-    packed = lax.fori_loop(0, PX // UNROLL, pack, (empty, empty, empty[:third], empty[:third]))
     for side in range(2):
         z_send[side, :PY, :] = packed[side]
-        z_send[side, PY:, :] = packed[2 + side]
+        z_send[side, PY:, :] = packed_mass[side]
     z_copies = [
         copy(z_send.at[side], z_recv.at[1 - side], side, z_sides[side]) for side in range(2)
     ]
@@ -456,11 +452,11 @@
             mass_rows = z_send[z_side, mass_at : mass_at + 8, :]
             for index in range(4):
                 if index < 3:
-                    source, at = rows, PITCH * index + 2 * x0
+                    source, at = rows, PITCH * index + 2 * x0 + CZ * z_side
                 else:
-                    source, at = mass_rows, PITCH * (tile // 3) + 2 * x0
+                    source, at = mass_rows, PITCH * (tile // 3) + 2 * x0 + CZ * z_side
                 to = start + 4 * index
-                moved = pltpu.roll(source, (LANES + to - at) % LANES, axis=1)
+                moved = pltpu.roll(source, (2 * LANES + to - at) % LANES, axis=1)
                 if result[half] is None:
                     result[half] = moved
                 else:
@@ -476,29 +472,43 @@
 
     for c in z_copies:
         c.wait()
-    low = (in_pitch < 2) & in_mom
-    high = (in_pitch >= CZ) & (in_pitch < CZ + 2) & in_mom
-    low3 = lane3 < 2
-    high3 = (lane3 >= CZ) & (lane3 < CZ + 2)
-
-    def unpack(step, carry):
-        for member in range(UNROLL):
-            x = UNROLL * step + member
-            at = pl.ds(pl.multiple_of(x * PY, 8), PY)
-            from_low = pltpu.roll(z_recv[0, :PY, :], LANES - 2 * x, axis=1)
-            from_high = pltpu.roll(z_recv[1, :PY, :], LANES + CZ - 2 * x, axis=1)
-            mom[at, :] += jnp.where(low, from_low, jnp.where(high, from_high, 0.0))
-            for part in range(3):
-                start = PITCH * part
-                rows = pl.ds(pl.multiple_of(x * PY + part * third, 8), third)
-                from_low = pltpu.roll(z_recv[0, PY:, :], 2 * LANES - start - 2 * x, axis=1)
-                from_high = pltpu.roll(
-                    z_recv[1, PY:, :], 2 * LANES + CZ - start - 2 * x, axis=1
-                )
-                mass[rows, :] += jnp.where(low3, from_low, jnp.where(high3, from_high, 0.0))
-        return carry
-
-    lax.fori_loop(0, PX // UNROLL, unpack, 0)
+    rim = in_mom & ((in_pitch < 2) | ((in_pitch >= CZ) & (in_pitch < CZ + 2)))
+    rim3 = (lane3 < 2) | ((lane3 >= CZ) & (lane3 < CZ + 2))
+    from_low = pltpu.roll(z_recv[0], 64, axis=1)
+    from_high = z_recv[1]
+    for x in range(PX):
+        at = slice(x * PY, (x + 1) * PY)
+        joined = jnp.where(pair == x, from_high[:PY], from_low[:PY])
+        moved = pltpu.roll(joined, (LANES + CZ - 2 * x) % LANES, axis=1)
+        mom[at, :] += jnp.where(rim, moved, 0.0)
+        for part in range(3):
+            start = PITCH * part
+            rows = slice(x * PY + part * third, x * PY + (part + 1) * third)
+            joined = jnp.where(pair3 == start // 2 + x, from_high[PY:], from_low[PY:])
+            moved = pltpu.roll(joined, (2 * LANES + CZ - start - 2 * x) % LANES, axis=1)
+            mass[rows, :] += jnp.where(rim3, moved, 0.0)
+
+    y_firsts = (0, CY)
+    for side in range(2):
+        y0 = y_firsts[side]
+        y_send[side, 0:PX, :] = mom[pl.ds(y0, PX, stride=PY), :]
+        y_send[side, PX : 2 * PX, :] = mom[pl.ds(y0 + 1, PX, stride=PY), :]
+        y_send[side, 2 * PX : 3 * PX, :] = mass[pl.ds(y0, PX, stride=PY), :] + pltpu.roll(
+            mass[pl.ds(y0 + 1, PX, stride=PY), :], 64, axis=1
+        )
+        y_send[side, 3 * PX :, :] = jnp.zeros((2, LANES), jnp.float32)
+    y_copies = [
+        copy(y_send.at[side], y_recv.at[1 - side], 4 + side, y_sides[side]) for side in range(2)
+    ]
+    for edge in range(4):
+        x0, y0 = CX * (edge // 2), y_firsts[edge % 2]
+        for layer in range(2):
+            at = (x0 + layer) * PY + y0
+            xy_send[edge, 2 * layer : 2 * layer + 2, :] = mom[at : at + 2, :]
+            xy_send[edge, 4 + 2 * layer : 6 + 2 * layer, :] = mass[at : at + 2, :]
+        y_copies.append(copy(xy_send.at[edge], xy_recv.at[3 - edge], 10 + edge, xy_sides[edge]))
+    for c in y_copies:
+        c.start()
 
     for c in xz_copies:
         c.wait()
@@ -537,21 +547,6 @@
                 moved = pltpu.roll(got, (LANES - PITCH * part) % LANES, axis=1)
                 mass[start : start + third, :] += jnp.where(near3, moved, 0.0)
     front = lane < 64
-
-    y_firsts = (0, CY)
-    for side in range(2):
-        y0 = y_firsts[side]
-        y_send[side, 0:PX, :] = mom[pl.ds(y0, PX, stride=PY), :]
-        y_send[side, PX : 2 * PX, :] = mom[pl.ds(y0 + 1, PX, stride=PY), :]
-        y_send[side, 2 * PX : 3 * PX, :] = mass[pl.ds(y0, PX, stride=PY), :] + pltpu.roll(
-            mass[pl.ds(y0 + 1, PX, stride=PY), :], 64, axis=1
-        )
-        y_send[side, 3 * PX :, :] = jnp.zeros((2, LANES), jnp.float32)
-    y_copies = [
-        copy(y_send.at[side], y_recv.at[1 - side], 4 + side, y_sides[side]) for side in range(2)
-    ]
-    for c in y_copies:
-        c.start()
     for c in y_copies:
         c.wait()
     for side in range(2):
@@ -563,6 +558,12 @@
         mom[at1, :] = mom[at1, :] + y_recv[side, PX : 2 * PX, :]
         mass[at0, :] = mass[at0, :] + jnp.where(front[:PX], got, 0.0)
         mass[at1, :] = mass[at1, :] + jnp.where(front[:PX], pltpu.roll(got, 64, axis=1), 0.0)
+    for edge in range(4):
+        x0, y0 = CX * (edge // 2), y_firsts[edge % 2]
+        for layer in range(2):
+            at = (x0 + layer) * PY + y0
+            mom[at : at + 2, :] += xy_recv[edge, 2 * layer : 2 * layer + 2, :]
+            mass[at : at + 2, :] += xy_recv[edge, 4 + 2 * layer : 6 + 2 * layer, :]
 
 
 def collect_kernel(
@@ -811,9 +812,11 @@
             pltpu.VMEM((4, 16, LANES), f32),
             pltpu.VMEM((2, 3 * PX + 2, LANES), f32),
             pltpu.VMEM((2, 3 * PX + 2, LANES), f32),
+            pltpu.VMEM((4, 8, LANES), f32),
+            pltpu.VMEM((4, 8, LANES), f32),
             pltpu.SemaphoreType.DMA((8,)),
-            pltpu.SemaphoreType.DMA((10,)),
-            pltpu.SemaphoreType.DMA((10,)),
+            pltpu.SemaphoreType.DMA((14,)),
+            pltpu.SemaphoreType.DMA((14,)),
         ],
         compiler_params=pltpu.CompilerParams(
             collective_id=0, has_side_effects=True, vmem_limit_bytes=VMEM_LIMIT

time: 33.1 us -> 27.4 us (0.83)
  Pallas kernels: 32.4 us -> 26.7 us
    pallas_call x1, Pallas kernels: 27.9 us -> 22.2 us  [shards(): pl.pallas_call(deposit_kernel, name='deposit', out_shape=(grid_shape, gri...]
where the time goes in v4:
time: 27.4 us; the launch traced here: 27.3 us
  Pallas kernels  26.7 us (97%)
  between operations  0.64 us (2%)
    pallas_call x1, Pallas kernels, shards(): pl.pallas_call(deposit_kernel, name='deposit', out_shape=(grid_shape, gri...  22.2 us
    pallas_call x1, Pallas kernels, shards(): pl.pallas_call(collect_kernel, name='collect', out_shape=(jax.ShapeDtypeS...  4.52 us

profile of v4, /device:TPU:1, one launch (start us, length us, event | category | flops | bytes accessed | tf_op | source)
XLA Modules:
  0.0 27.3 jit_solution(7285322005163187883)
XLA Ops:
  0.6 22.2 %deposit.1 = (f32[1296,128]{1,0:T(8,128)S(1)}, f32[1296,128]{1,0:T(8,128)S(1)}, f32[704,128]{1,0:T(8,128)S(1)}, f32[192,128]{1,0:T(8,128)S(1)}) custom-call(s32[32]{0:T(128)} %tile_hbm.3, s32[32]{0:T(128)} %count_hbm.1, f32[3,4096]{1,0:T(4,128)} %frac_hbm.1, s32[3,4096]{1,0:T(4,128)} %offset_hbm.1, f32[3,4096]{1,0:T(4,128)} %velocity_hbm.1, ...), custom_call_target="tpu_custom_call" | custom-call | tf_op jit(solution)/shard_map/deposit/pallas_call | solution.py:783
  22.8 4.5 %collect.1 = (f32[3,4096]{1,0:T(4,128)}, f32[9,4096]{1,0:T(8,128)}, f32[6,4096]{1,0:T(8,128)}, f32[3,16,32,64]{3,2,1,0:T(8,128)}) custom-call(s32[32]{0:T(128)} %tile_hbm.3, f32[1296,128]{1,0:T(8,128)S(1)} %get-tuple-element.12.mom_ref, f32[1296,128]{1,0:T(8,128)S(1)} %get-tuple-element.13.mass_ref, f32[704,128]{1,0:T(8,128)S(1)} %get-tuple-element.14.shared_ref, ...), custom_call_target="tpu_custom_call" | custom-call | tf_op jit(solution)/shard_map/collect/pallas_call | solution.py:825

commit v5 on v4

--- a/solution.py
+++ b/solution.py
@@ -127,10 +127,14 @@
     affine_hbm,
     stress_hbm,
     mass_hbm,
+    velocity_out,
+    collect_high,
+    collect_low,
+    y_table,
+    stress_out,
     mom,
     mass,
     shared_ref,
-    stress_out,
     tile_ref,
     count_ref,
     frac_ref,
@@ -164,9 +168,10 @@
         for axis, step in zip(axes, (dx, dy, dz)):
             size = lax.axis_size(axis)
             moved = lax.axis_index(axis)
-            if step:
-                moved = moved + step
-                moved = jnp.where(moved < 0, size - 1, jnp.where(moved >= size, 0, moved))
+            if step and size & (size - 1) == 0:
+                moved = (moved + size + step) & (size - 1)
+            elif step:
+                moved = lax.rem(moved + size + step, size)
             place.append(moved)
         return tuple(place)
 
@@ -265,13 +270,14 @@
     for index in range(5):
         put(T_LY + index, spline[1][index])
         put(T_LZ + index, spline[2][index])
+        y_table[index * blocks : (index + 1) * blocks, :] = spline[1][index]
 
     lanes = lax.broadcasted_iota(jnp.int32, (8, 32), 1)
     channel = [(lanes >= 8 * index) & (lanes < 8 * index + 8) for index in range(4)]
     rest = jnp.zeros((8, LANES - 32), jnp.float32)
     blank = jnp.zeros((8, LANES), jnp.float32)
 
-    def block_sums(block):
+    def row_of(block):
         def row(index):
             if index < T_SHARED:
                 value = shared_ref[pl.ds(index * blocks + block, 1), :]
@@ -279,6 +285,10 @@
                 value = table[pl.ds((index - T_SHARED) * blocks + block, 1), :]
             return jnp.broadcast_to(value, (8, LANES))
 
+        return row
+
+    def block_sums(block):
+        row = row_of(block)
         wy, wyd = axis_weights(row, T_LY, T_MY, T_RY, T_OY, T_Y)
         wz, wzd = axis_weights(row, T_LZ, T_MZ, T_RZ, T_OZ, T_Z)
         wx = [row(T_WX + node) for node in range(6)]
@@ -510,6 +520,68 @@
     for c in y_copies:
         c.start()
 
+    width_x = lax.axis_size("gx") * CX
+    height_y = lax.axis_size("gy") * CY
+    depth_z = lax.axis_size("gz") * CZ
+    first_z = lax.axis_index("gz") * CZ
+    first_y = lax.axis_index("gy") * CY
+    first_x = lax.axis_index("gx") * CX
+    z_index = lax.rem(lane - 2 * PITCH - 1 + first_z + depth_z, depth_z)
+    is_y = (lane >= PITCH) & (lane < 2 * PITCH)
+    is_z = (lane >= 2 * PITCH) & (lane < 3 * PITCH)
+    z_floor = is_z & (z_index < 2)
+    z_top = is_z & (z_index >= depth_z - 2)
+    fall = jnp.where(is_y, time_step * gravity, 0.0)
+    row_index = lax.broadcasted_iota(jnp.int32, (PY, LANES), 0)
+    y_floor = is_y & (lax.rem(row_index - 1 + first_y + height_y, height_y) < 2)
+
+    def update(mom_values, mass_values, floor, count):
+        inverse = 1.0 / (mass_values + mass_floor)
+        inverse = jnp.where(
+            lane[:count] < PITCH,
+            inverse,
+            jnp.where(
+                is_y[:count],
+                pltpu.roll(inverse, PITCH, axis=1),
+                pltpu.roll(inverse, 2 * PITCH, axis=1),
+            ),
+        )
+        values = mom_values * inverse - fall[:count]
+        values = jnp.where(z_floor[:count] | floor, jnp.maximum(values, 0.0), values)
+        return jnp.where(z_top[:count], jnp.minimum(values, 0.0), values)
+
+    def off_outlet(x):
+        x_index = lax.rem(first_x + x - 1 + width_x, width_x)
+        return (x_index < width_x // 4) | (x_index >= width_x - width_x // 4)
+
+    def update_layer(x):
+        at = pl.ds(pl.multiple_of(x * PY, 8), PY)
+        velocity_out[at, :] = update(mom[at, :], mass[at, :], y_floor & off_outlet(x), PY)
+
+    def layers(step, carry):
+        for member in range(7):
+            update_layer(2 + 7 * step + member)
+        return carry
+
+    lax.fori_loop(0, 2, layers, 0)
+
+    def right_sides(step, carry):
+        for member in range(2):
+            block = 2 * step + member
+            row = row_of(block)
+            wz, wzd = axis_weights(row, T_LZ, T_MZ, T_RZ, T_OZ, T_Z)
+            wx = [row(T_WX + node) for node in range(6)]
+            wxd = [row(T_WXD + node) for node in range(6)]
+            at = pl.ds(pl.multiple_of(48 * block, 16), 48)
+            for index, (along_x, along_z) in enumerate(((wx, wz), (wxd, wz), (wx, wzd))):
+                high, low = split(jnp.concatenate([w * along_z for w in along_x], axis=0))
+                cols = slice(index * LANES, (index + 1) * LANES)
+                collect_high[at, cols] = high
+                collect_low[at, cols] = low
+        return carry
+
+    lax.fori_loop(0, blocks // 2, right_sides, 0)
+
     for c in xz_copies:
         c.wait()
     lane8 = lane[:8]
@@ -546,6 +618,8 @@
                 start = first + layer * PY + part * third
                 moved = pltpu.roll(got, (LANES - PITCH * part) % LANES, axis=1)
                 mass[start : start + third, :] += jnp.where(near3, moved, 0.0)
+    for x in (0, 1, CX, CX + 1):
+        update_layer(x)
     front = lane < 64
     for c in y_copies:
         c.wait()
@@ -564,13 +638,22 @@
             at = (x0 + layer) * PY + y0
             mom[at : at + 2, :] += xy_recv[edge, 2 * layer : 2 * layer + 2, :]
             mass[at : at + 2, :] += xy_recv[edge, 4 + 2 * layer : 6 + 2 * layer, :]
+    x_rows = lax.broadcasted_iota(jnp.int32, (PX, LANES), 0)
+    outside = off_outlet(x_rows)
+    for y in (0, 1, CY, CY + 1):
+        at = pl.ds(y, PX, stride=PY)
+        on_floor = lax.rem(first_y + (y - 1 + height_y), height_y) < 2
+        velocity_out[at, :] = update(
+            mom[at, :], mass[at, :], is_y[:PX] & outside & on_floor, PX
+        )
 
 
 def collect_kernel(
     tile_hbm,
-    mom_ref,
-    mass_ref,
-    shared_ref,
+    velocity,
+    right_high,
+    right_low,
+    y_table,
     stress_in,
     new_velocity_ref,
     new_affine_ref,
@@ -579,7 +662,6 @@
     tile_ref,
     new_stress_ref,
     grid_velocity_ref,
-    velocity,
     partial,
     final,
     copy_sem,
@@ -593,50 +675,6 @@
         ]
     stress_copy = pltpu.make_async_copy(new_stress_ref, new_stress_hbm, copy_sem.at[1])
     stress_copy.start()
-    width_x = lax.axis_size("gx") * CX
-    height_y = lax.axis_size("gy") * CY
-    depth_z = lax.axis_size("gz") * CZ
-    lane = lax.broadcasted_iota(jnp.int32, (PY, LANES), 1)
-    row_index = lax.broadcasted_iota(jnp.int32, (PY, LANES), 0)
-    first_z = lax.axis_index("gz") * CZ
-    first_y = lax.axis_index("gy") * CY
-    first_x = lax.axis_index("gx") * CX
-    z_index = lax.rem(lane - 2 * PITCH - 1 + first_z + depth_z, depth_z)
-    y_index = lax.rem(row_index - 1 + first_y + height_y, height_y)
-    is_y = (lane >= PITCH) & (lane < 2 * PITCH)
-    is_z = (lane >= 2 * PITCH) & (lane < 3 * PITCH)
-    z_floor = is_z & (z_index < 2)
-    z_top = is_z & (z_index >= depth_z - 2)
-    y_floor = is_y & (y_index < 2)
-    fall = jnp.where(is_y, time_step * gravity, 0.0)
-
-    def layer(x):
-        at = pl.ds(pl.multiple_of(x * PY, 8), PY)
-        x_index = lax.rem(first_x + x - 1 + width_x, width_x)
-        outlet = (x_index >= width_x // 4) & (x_index < width_x - width_x // 4)
-        inverse = 1.0 / (mass_ref[at, :] + mass_floor)
-        inverse = jnp.where(
-            lane < PITCH,
-            inverse,
-            jnp.where(
-                is_y, pltpu.roll(inverse, PITCH, axis=1), pltpu.roll(inverse, 2 * PITCH, axis=1)
-            ),
-        )
-        values = mom_ref[at, :] * inverse - fall
-        lifted = jnp.maximum(values, 0.0)
-        values = jnp.where(
-            z_floor | (y_floor & jnp.logical_not(outlet)), lifted, values
-        )
-        values = jnp.where(z_top, jnp.minimum(values, 0.0), values)
-        velocity[at, :] = values
-
-    def layers(step, carry):
-        for member in range(3):
-            layer(3 * step + member)
-        return carry
-
-    lax.fori_loop(0, PX // 3, layers, 0)
-
     def output(step, carry):
         for member in range(4):
             x = 4 * step + member
@@ -651,12 +689,6 @@
     tile_copy.wait()
 
     lanes = lax.broadcasted_iota(jnp.int32, (8, LANES), 1)
-
-    def row_of(block):
-        def row(index):
-            return jnp.broadcast_to(shared_ref[pl.ds(index * blocks + block, 1), :], (8, LANES))
-
-        return row
 
     def gather(block):
         tile_x, tile_y, tile_z = tile_coords(tile_ref, block)
@@ -678,33 +710,24 @@
         return jnp.concatenate(rows, axis=0)
 
     def contract(block, left_side):
-        row = row_of(block)
-        wz, wzd = axis_weights(row, T_LZ, T_MZ, T_RZ, T_OZ, T_Z)
-        wx = [row(T_WX + node) for node in range(6)]
-        wxd = [row(T_WXD + node) for node in range(6)]
-        right_side = jnp.concatenate(
-            [
-                jnp.concatenate([w * wz for w in wx], axis=0),
-                jnp.concatenate([w * wz for w in wxd], axis=0),
-                jnp.concatenate([w * wzd for w in wx], axis=0),
-            ],
-            axis=1,
-        )
         left_high, left_low = split(left_side[:, :48])
-        right_high, right_low = split(right_side)
+        at = pl.ds(pl.multiple_of(48 * block, 16), 48)
         both = jnp.dot(
             jnp.concatenate([left_high, left_low], axis=0),
-            right_high,
+            right_high[at, :],
             preferred_element_type=jnp.float32,
         )
         return (
             both[:24]
             + both[24:]
-            + jnp.dot(left_high, right_low, preferred_element_type=jnp.float32)
+            + jnp.dot(left_high, right_low[at, :], preferred_element_type=jnp.float32)
         )
 
     def weigh(block, sums):
-        wy, wyd = axis_weights(row_of(block), T_LY, T_MY, T_RY, T_OY, T_Y)
+        def row(index):
+            return jnp.broadcast_to(y_table[pl.ds(index * blocks + block, 1), :], (8, LANES))
+
+        wy, wyd = axis_weights(row, 0, 1, 2, 3, 4)
         for dim in range(3):
             part = sums[8 * dim : 8 * dim + 8]
             terms = (
@@ -780,18 +803,23 @@
             point_mass.reshape(blocks, BLOCK),
         )
     ]
-    mom, mass, shared, stress = pl.pallas_call(
+    right_shape = jax.ShapeDtypeStruct((48 * blocks, 3 * LANES), jnp.bfloat16)
+    velocity, right_high, right_low, y_table, stress = pl.pallas_call(
         deposit_kernel,
         name="deposit",
         out_shape=(
             grid_shape,
-            grid_shape,
-            jax.ShapeDtypeStruct((T_SHARED * blocks, LANES), f32),
+            right_shape,
+            right_shape,
+            jax.ShapeDtypeStruct((5 * blocks, LANES), f32),
             jax.ShapeDtypeStruct((6 * blocks, LANES), f32),
         ),
         in_specs=[hbm] * 8,
-        out_specs=(vmem,) * 4,
+        out_specs=(vmem,) * 5,
         scratch_shapes=[
+            pltpu.VMEM((ROWS, LANES), f32),
+            pltpu.VMEM((ROWS, LANES), f32),
+            pltpu.VMEM((T_SHARED * blocks, LANES), f32),
             pltpu.SMEM((blocks,), jnp.int32),
             pltpu.SMEM((blocks,), jnp.int32),
             pltpu.VMEM((3, points), f32),
@@ -831,19 +859,18 @@
             jax.ShapeDtypeStruct((6, points), f32),
             jax.ShapeDtypeStruct((3, CX, CZ, CY), f32),
         ),
-        in_specs=[hbm] + [vmem] * 4,
+        in_specs=[hbm] + [vmem] * 5,
         out_specs=(vmem, vmem, hbm, hbm),
         scratch_shapes=[
             pltpu.SMEM((blocks,), jnp.int32),
             pltpu.VMEM((6, points), f32),
             pltpu.VMEM((3, CX, CZ, CY), f32),
-            pltpu.VMEM((ROWS, LANES), f32),
             pltpu.VMEM((12 * 8 * blocks, LANES), f32),
             pltpu.VMEM((12 * blocks, LANES), f32),
             pltpu.SemaphoreType.DMA((3,)),
         ],
         compiler_params=pltpu.CompilerParams(vmem_limit_bytes=VMEM_LIMIT),
-    )(arguments[0], mom, mass, shared, stress)
+    )(arguments[0], velocity, right_high, right_low, y_table, stress)
     return (new_velocity, new_affine, new_stress, jnp.swapaxes(grid_velocity, 2, 3))
 
 

time: 27.4 us -> 26.6 us (0.971)
  Pallas kernels: 26.7 us -> 25.9 us
    pallas_call x1, Pallas kernels: 4.52 us -> 3.63 us  [shards(): pl.pallas_call(collect_kernel, name='collect', out_shape=(jax.ShapeDtypeS...]
where the time goes in v5:
time: 26.6 us; the launch traced here: 26.5 us
  Pallas kernels  25.9 us (97%)
  between operations  0.64 us (2%)
    pallas_call x1, Pallas kernels, shards(): pl.pallas_call(deposit_kernel, name='deposit', out_shape=(grid_shape, rig...  22.3 us
    pallas_call x1, Pallas kernels, shards(): pl.pallas_call(collect_kernel, name='collect', out_shape=(jax.ShapeDtypeS...  3.63 us

profile of v5, /device:TPU:1, one launch (start us, length us, event | category | flops | bytes accessed | tf_op | source)
XLA Modules:
  0.0 26.5 jit_solution(9493094032947035575)
XLA Ops:
  0.6 22.3 %deposit.1 = (f32[1296,128]{1,0:T(8,128)S(1)}, bf16[1536,384]{1,0:T(8,128)(2,1)S(1)}, bf16[1536,384]{1,0:T(8,128)(2,1)S(1)}, f32[160,128]{1,0:T(8,128)S(1)}, f32[192,128]{1,0:T(8,128)S(1)}) custom-call(s32[32]{0:T(128)} %tile_hbm.3, s32[32]{0:T(128)} %count_hbm.1, f32[3,4096]{1,0:T(4,128)} %frac_hbm.1, s32[3,4096]{1,0:T(4,128)} %offset_hbm.1, ...), custom_call_target="tpu_custom_call" | custom-call | tf_op jit(solution)/shard_map/deposit/pallas_call | solution.py:807
  22.9 3.6 %collect.1 = (f32[3,4096]{1,0:T(4,128)}, f32[9,4096]{1,0:T(8,128)}, f32[6,4096]{1,0:T(8,128)}, f32[3,16,32,64]{3,2,1,0:T(8,128)}) custom-call(s32[32]{0:T(128)} %tile_hbm.3, f32[1296,128]{1,0:T(8,128)S(1)} %get-tuple-element.13.velocity, bf16[1536,384]{1,0:T(8,128)(2,1)S(1)} %get-tuple-element.14.right_high, ...), custom_call_target="tpu_custom_call" | custom-call | tf_op jit(solution)/shard_map/collect/pallas_call | solution.py:853

commit v6 on v5

--- a/solution.py
+++ b/solution.py
@@ -31,7 +31,7 @@
 PITCH = 40
 LANES = 128
 ROWS = PX * PY
-GROUP = 4
+GROUP = 16
 VMEM_LIMIT = 16 * 1024 * 1024
 MESH = pl.DeviceIdType.MESH
 

time: 26.6 us -> 25.8 us (0.970)
  Pallas kernels: 25.9 us -> 25.1 us
    pallas_call x1, Pallas kernels: 3.63 us -> 2.52 us  [shards(): pl.pallas_call(collect_kernel, name='collect', out_shape=(jax.ShapeDtypeS...]
    pallas_call x1, Pallas kernels: 22.3 us -> 22.5 us  [shards(): pl.pallas_call(deposit_kernel, name='deposit', out_shape=(grid_shape, rig...]
where the time goes in v6:
time: 25.8 us; the launch traced here: 25.7 us
  Pallas kernels  25.1 us (97%)
  between operations  0.64 us (2%)
    pallas_call x1, Pallas kernels, shards(): pl.pallas_call(deposit_kernel, name='deposit', out_shape=(grid_shape, rig...  22.5 us
    pallas_call x1, Pallas kernels, shards(): pl.pallas_call(collect_kernel, name='collect', out_shape=(jax.ShapeDtypeS...  2.52 us

profile of v6, /device:TPU:1, one launch (start us, length us, event | category | flops | bytes accessed | tf_op | source)
XLA Modules:
  0.0 25.7 jit_solution(11089675770489815653)
XLA Ops:
  0.6 22.5 %deposit.1 = (f32[1296,128]{1,0:T(8,128)S(1)}, bf16[1536,384]{1,0:T(8,128)(2,1)S(1)}, bf16[1536,384]{1,0:T(8,128)(2,1)S(1)}, f32[160,128]{1,0:T(8,128)S(1)}, f32[192,128]{1,0:T(8,128)S(1)}) custom-call(s32[32]{0:T(128)} %tile_hbm.3, s32[32]{0:T(128)} %count_hbm.1, f32[3,4096]{1,0:T(4,128)} %frac_hbm.1, s32[3,4096]{1,0:T(4,128)} %offset_hbm.1, ...), custom_call_target="tpu_custom_call" | custom-call | tf_op jit(solution)/shard_map/deposit/pallas_call | solution.py:807
  23.2 2.5 %collect.1 = (f32[3,4096]{1,0:T(4,128)}, f32[9,4096]{1,0:T(8,128)}, f32[6,4096]{1,0:T(8,128)}, f32[3,16,32,64]{3,2,1,0:T(8,128)}) custom-call(s32[32]{0:T(128)} %tile_hbm.3, f32[1296,128]{1,0:T(8,128)S(1)} %get-tuple-element.13.velocity, bf16[1536,384]{1,0:T(8,128)(2,1)S(1)} %get-tuple-element.14.right_high, ...), custom_call_target="tpu_custom_call" | custom-call | tf_op jit(solution)/shard_map/collect/pallas_call | solution.py:853

commit v7 on v6

--- a/solution.py
+++ b/solution.py
@@ -147,8 +147,10 @@
     table,
     placed_high,
     placed_low,
-    z_send,
-    z_recv,
+    za_send,
+    za_recv,
+    zb_send,
+    zb_recv,
     x_send,
     x_recv,
     xz_send,
@@ -403,6 +405,58 @@
     lane3 = lane[:third]
     pl.semaphore_wait(barrier, 14)
 
+    pair = jnp.where(in_mom, in_pitch >> 1, -1)
+    far = lax.rem(lane + (LANES - CZ), LANES)
+    far_pair = jnp.where(far < 3 * PITCH, lax.rem(far, PITCH) >> 1, -1)
+    pair3 = lane3 >> 1
+    far_pair3 = far[:third] >> 1
+    outer = (0, CY)
+    groups = (8, 8 + third, PY - third)
+
+    def pick(values, start, x, whole):
+        shift = start + 2 * x
+        moved = pltpu.roll(values, shift, axis=1) if shift else values
+        count = values.shape[0]
+        sides = (pair, far_pair) if whole else (pair3, far_pair3)
+        return [(side[:count] == shift // 2 if not whole else side[:count] == x, moved)
+                for side in sides]
+
+    def gather_pairs(pieces, whole):
+        result = [None, None]
+        for values, start, x in pieces:
+            for side, (mask, moved) in enumerate(pick(values, start, x, whole)):
+                before = 0.0 if result[side] is None else result[side]
+                result[side] = jnp.where(mask, moved, before)
+        return result
+
+    def layer_rows(grid, x, first, count):
+        return grid[x * PY + first : x * PY + first + count, :]
+
+    def z_start(send, recv, slot):
+        copies = [
+            copy(send.at[side], recv.at[1 - side], slot + side, z_sides[side])
+            for side in range(2)
+        ]
+        for c in copies:
+            c.start()
+        return copies
+
+    for index, first in enumerate(outer):
+        packed = gather_pairs([(layer_rows(mom, x, first, 8), 0, x) for x in range(PX)], True)
+        for side in range(2):
+            za_send[side, 8 * index : 8 * index + 8, :] = packed[side]
+    packed = gather_pairs(
+        [
+            (layer_rows(mass, x, first, 8), PITCH * index, x)
+            for index, first in enumerate(outer)
+            for x in range(PX)
+        ],
+        False,
+    )
+    for side in range(2):
+        za_send[side, 16:, :] = packed[side]
+    za_copies = z_start(za_send, za_recv, 0)
+
     firsts = (0, CX * PY)
     for side in range(2):
         first = firsts[side]
@@ -421,35 +475,19 @@
     for c in x_copies:
         c.start()
 
-    pair = jnp.where(in_mom, in_pitch >> 1, -1)
-    far = lax.rem(lane + (LANES - CZ), LANES)
-    far_pair = jnp.where(far < 3 * PITCH, lax.rem(far, PITCH) >> 1, -1)
-    pair3 = lane3 >> 1
-    far_pair3 = far[:third] >> 1
-    packed, packed_mass = [None, None], [None, None]
-    for x in range(PX):
-        at = slice(x * PY, (x + 1) * PY)
-        moved = pltpu.roll(mom[at, :], 2 * x, axis=1) if x else mom[at, :]
-        for side, which in enumerate((pair, far_pair)):
-            packed[side] = jnp.where(which == x, moved, packed[side] if x else 0.0)
-        for part in range(3):
-            start = PITCH * part
-            rows = slice(x * PY + part * third, x * PY + (part + 1) * third)
-            moved = mass[rows, :]
-            if start + 2 * x:
-                moved = pltpu.roll(moved, start + 2 * x, axis=1)
-            for side, which in enumerate((pair3, far_pair3)):
-                packed_mass[side] = jnp.where(
-                    which == start // 2 + x, moved, packed_mass[side] if start + x else 0.0
-                )
+    packed = gather_pairs([(layer_rows(mom, x, 8, CY - 8), 0, x) for x in range(PX)], True)
+    packed_mass = gather_pairs(
+        [
+            (layer_rows(mass, x, first, third), PITCH * index, x)
+            for index, first in enumerate(groups)
+            for x in range(PX)
+        ],
+        False,
+    )
     for side in range(2):
-        z_send[side, :PY, :] = packed[side]
-        z_send[side, PY:, :] = packed_mass[side]
-    z_copies = [
-        copy(z_send.at[side], z_recv.at[1 - side], side, z_sides[side]) for side in range(2)
-    ]
-    for c in z_copies:
-        c.start()
+        zb_send[side, : CY - 8, :] = packed[side]
+        zb_send[side, CY - 8 :, :] = packed_mass[side]
+    zb_copies = z_start(zb_send, zb_recv, 14)
 
     quad = lax.broadcasted_iota(jnp.int32, (8, LANES), 1) >> 2
     for edge in range(4):
@@ -457,14 +495,20 @@
         result = [None, None]
         for tile in range(PY // 8):
             half, start = tile // 8, 16 * (tile % 8)
-            rows = z_send[z_side, 8 * tile : 8 * tile + 8, :]
-            mass_at = PY + 8 * (tile % 3)
-            mass_rows = z_send[z_side, mass_at : mass_at + 8, :]
+            if 8 * tile in outer:
+                z_buffer, mom_at, mass_at = za_send, tile, 16
+                mass_group = outer.index(8 * tile)
+            else:
+                mass_group = min((tile - 1) // 3, 2)
+                z_buffer, mom_at = zb_send, 8 * (tile - 1)
+                mass_at = CY - 8 + 8 * tile - groups[mass_group]
+            rows = z_buffer[z_side, mom_at : mom_at + 8, :]
+            mass_rows = z_buffer[z_side, mass_at : mass_at + 8, :]
             for index in range(4):
                 if index < 3:
                     source, at = rows, PITCH * index + 2 * x0 + CZ * z_side
                 else:
-                    source, at = mass_rows, PITCH * (tile // 3) + 2 * x0 + CZ * z_side
+                    source, at = mass_rows, PITCH * mass_group + 2 * x0 + CZ * z_side
                 to = start + 4 * index
                 moved = pltpu.roll(source, (2 * LANES + to - at) % LANES, axis=1)
                 if result[half] is None:
@@ -480,23 +524,26 @@
     for c in xz_copies:
         c.start()
 
-    for c in z_copies:
-        c.wait()
     rim = in_mom & ((in_pitch < 2) | ((in_pitch >= CZ) & (in_pitch < CZ + 2)))
     rim3 = (lane3 < 2) | ((lane3 >= CZ) & (lane3 < CZ + 2))
-    from_low = pltpu.roll(z_recv[0], 64, axis=1)
-    from_high = z_recv[1]
+
+    def spread(grid, x, first, count, received, start, whole):
+        low, high = received
+        mask = pair[:count] == x if whole else pair3[:count] == start // 2 + x
+        moved = pltpu.roll(
+            jnp.where(mask, high, low), (2 * LANES + CZ - start - 2 * x) % LANES, axis=1
+        )
+        at = slice(x * PY + first, x * PY + first + count)
+        grid[at, :] += jnp.where((rim if whole else rim3)[:count], moved, 0.0)
+
+    for c in za_copies:
+        c.wait()
+    received = pltpu.roll(za_recv[0], 64, axis=1), za_recv[1]
     for x in range(PX):
-        at = slice(x * PY, (x + 1) * PY)
-        joined = jnp.where(pair == x, from_high[:PY], from_low[:PY])
-        moved = pltpu.roll(joined, (LANES + CZ - 2 * x) % LANES, axis=1)
-        mom[at, :] += jnp.where(rim, moved, 0.0)
-        for part in range(3):
-            start = PITCH * part
-            rows = slice(x * PY + part * third, x * PY + (part + 1) * third)
-            joined = jnp.where(pair3 == start // 2 + x, from_high[PY:], from_low[PY:])
-            moved = pltpu.roll(joined, (2 * LANES + CZ - start - 2 * x) % LANES, axis=1)
-            mass[rows, :] += jnp.where(rim3, moved, 0.0)
+        for index, first in enumerate(outer):
+            rows = slice(8 * index, 8 * index + 8)
+            spread(mom, x, first, 8, [side[rows] for side in received], 0, True)
+            spread(mass, x, first, 8, [side[16:] for side in received], PITCH * index, False)
 
     y_firsts = (0, CY)
     for side in range(2):
@@ -519,6 +566,20 @@
         y_copies.append(copy(xy_send.at[edge], xy_recv.at[3 - edge], 10 + edge, xy_sides[edge]))
     for c in y_copies:
         c.start()
+
+    for c in zb_copies:
+        c.wait()
+    received = pltpu.roll(zb_recv[0], 64, axis=1), zb_recv[1]
+    for x in range(PX):
+        spread(mom, x, 8, CY - 8, [side[: CY - 8] for side in received], 0, True)
+        for index, first in enumerate(groups):
+            skip = 0 if index < 2 else 8
+            count = third if index < 2 else 8
+            rows = slice(CY - 8 + skip, CY - 8 + skip + count)
+            spread(
+                mass, x, first + skip, count, [side[rows] for side in received],
+                PITCH * index, False,
+            )
 
     width_x = lax.axis_size("gx") * CX
     height_y = lax.axis_size("gy") * CY
@@ -832,8 +893,10 @@
             pltpu.VMEM(((T_ALL - T_SHARED) * blocks, LANES), f32),
             pltpu.VMEM((6, 8 * blocks, 2 * LANES), jnp.bfloat16),
             pltpu.VMEM((6, 8 * blocks, 2 * LANES), jnp.bfloat16),
-            pltpu.VMEM((2, face, LANES), f32),
-            pltpu.VMEM((2, face, LANES), f32),
+            pltpu.VMEM((2, 24, LANES), f32),
+            pltpu.VMEM((2, 24, LANES), f32),
+            pltpu.VMEM((2, CY - 8 + PY // 3, LANES), f32),
+            pltpu.VMEM((2, CY - 8 + PY // 3, LANES), f32),
             pltpu.VMEM((2, 2 * face, LANES), f32),
             pltpu.VMEM((2, 2 * face, LANES), f32),
             pltpu.VMEM((4, 16, LANES), f32),
@@ -843,8 +906,8 @@
             pltpu.VMEM((4, 8, LANES), f32),
             pltpu.VMEM((4, 8, LANES), f32),
             pltpu.SemaphoreType.DMA((8,)),
-            pltpu.SemaphoreType.DMA((14,)),
-            pltpu.SemaphoreType.DMA((14,)),
+            pltpu.SemaphoreType.DMA((16,)),
+            pltpu.SemaphoreType.DMA((16,)),
         ],
         compiler_params=pltpu.CompilerParams(
             collective_id=0, has_side_effects=True, vmem_limit_bytes=VMEM_LIMIT

time: 25.8 us -> 26.2 us (1.016)
  Pallas kernels: 25.1 us -> 25.4 us
    pallas_call x1, Pallas kernels: 22.5 us -> 22.9 us  [shards(): pl.pallas_call(deposit_kernel, name='deposit', out_shape=(grid_shape, rig...]
where the time goes in v7:
time: 26.2 us; the launch traced here: 26.1 us
  Pallas kernels  25.4 us (97%)
  between operations  0.64 us (2%)
    pallas_call x1, Pallas kernels, shards(): pl.pallas_call(deposit_kernel, name='deposit', out_shape=(grid_shape, rig...  22.9 us
    pallas_call x1, Pallas kernels, shards(): pl.pallas_call(collect_kernel, name='collect', out_shape=(jax.ShapeDtypeS...  2.52 us

profile of v7, /device:TPU:1, one launch (start us, length us, event | category | flops | bytes accessed | tf_op | source)
XLA Modules:
  0.0 26.1 jit_solution(16064154482322643282)
XLA Ops:
  0.6 22.9 %deposit.1 = (f32[1296,128]{1,0:T(8,128)S(1)}, bf16[1536,384]{1,0:T(8,128)(2,1)S(1)}, bf16[1536,384]{1,0:T(8,128)(2,1)S(1)}, f32[160,128]{1,0:T(8,128)S(1)}, f32[192,128]{1,0:T(8,128)S(1)}) custom-call(s32[32]{0:T(128)} %tile_hbm.3, s32[32]{0:T(128)} %count_hbm.1, f32[3,4096]{1,0:T(4,128)} %frac_hbm.1, s32[3,4096]{1,0:T(4,128)} %offset_hbm.1, ...), custom_call_target="tpu_custom_call" | custom-call | tf_op jit(solution)/shard_map/deposit/pallas_call | solution.py:868
  23.5 2.5 %collect.1 = (f32[3,4096]{1,0:T(4,128)}, f32[9,4096]{1,0:T(8,128)}, f32[6,4096]{1,0:T(8,128)}, f32[3,16,32,64]{3,2,1,0:T(8,128)}) custom-call(s32[32]{0:T(128)} %tile_hbm.3, f32[1296,128]{1,0:T(8,128)S(1)} %get-tuple-element.13.velocity, bf16[1536,384]{1,0:T(8,128)(2,1)S(1)} %get-tuple-element.14.right_high, ...), custom_call_target="tpu_custom_call" | custom-call | tf_op jit(solution)/shard_map/collect/pallas_call | solution.py:916

commit v8 on v7

--- a/solution.py
+++ b/solution.py
@@ -405,6 +405,25 @@
     lane3 = lane[:third]
     pl.semaphore_wait(barrier, 14)
 
+    firsts = (0, CX * PY)
+    used = CY + 2
+    short = used // 3
+    for side in range(2):
+        for layer in range(2):
+            start = firsts[side] + layer * PY
+            x_send[side, layer * used : (layer + 1) * used, :] = mom[start : start + used, :]
+            at = 2 * used + layer * short
+            x_send[side, at : at + short, :] = (
+                mass[start : start + short, :]
+                + pltpu.roll(mass[start + short : start + 2 * short, :], PITCH, axis=1)
+                + pltpu.roll(mass[start + 2 * short : start + 3 * short, :], 2 * PITCH, axis=1)
+            )
+    x_copies = [
+        copy(x_send.at[side], x_recv.at[1 - side], 2 + side, x_sides[side]) for side in range(2)
+    ]
+    for c in x_copies:
+        c.start()
+
     pair = jnp.where(in_mom, in_pitch >> 1, -1)
     far = lax.rem(lane + (LANES - CZ), LANES)
     far_pair = jnp.where(far < 3 * PITCH, lax.rem(far, PITCH) >> 1, -1)
@@ -456,24 +475,6 @@
     for side in range(2):
         za_send[side, 16:, :] = packed[side]
     za_copies = z_start(za_send, za_recv, 0)
-
-    firsts = (0, CX * PY)
-    for side in range(2):
-        first = firsts[side]
-        x_send[side, : 2 * PY, :] = mom[first : first + 2 * PY, :]
-        for layer in range(2):
-            start = first + layer * PY
-            at = 2 * PY + layer * third
-            x_send[side, at : at + third, :] = (
-                mass[start : start + third, :]
-                + pltpu.roll(mass[start + third : start + 2 * third, :], PITCH, axis=1)
-                + pltpu.roll(mass[start + 2 * third : start + 3 * third, :], 2 * PITCH, axis=1)
-            )
-    x_copies = [
-        copy(x_send.at[side], x_recv.at[1 - side], 2 + side, x_sides[side]) for side in range(2)
-    ]
-    for c in x_copies:
-        c.start()
 
     packed = gather_pairs([(layer_rows(mom, x, 8, CY - 8), 0, x) for x in range(PX)], True)
     packed_mass = gather_pairs(
@@ -668,17 +669,17 @@
 
     for c in x_copies:
         c.wait()
-    near3 = lane3 < PITCH
+    near = lane[:short] < PITCH
     for side in range(2):
-        first = firsts[side]
-        mom[first : first + 2 * PY, :] += x_recv[side, : 2 * PY, :]
         for layer in range(2):
-            at = 2 * PY + layer * third
-            got = x_recv[side, at : at + third, :]
+            start = firsts[side] + layer * PY
+            mom[start : start + used, :] += x_recv[side, layer * used : (layer + 1) * used, :]
+            at = 2 * used + layer * short
+            got = x_recv[side, at : at + short, :]
             for part in range(3):
-                start = first + layer * PY + part * third
-                moved = pltpu.roll(got, (LANES - PITCH * part) % LANES, axis=1)
-                mass[start : start + third, :] += jnp.where(near3, moved, 0.0)
+                first = start + part * short
+                moved = pltpu.roll(got, LANES - PITCH * part, axis=1) if part else got
+                mass[first : first + short, :] += jnp.where(near, moved, 0.0)
     for x in (0, 1, CX, CX + 1):
         update_layer(x)
     front = lane < 64
@@ -897,8 +898,8 @@
             pltpu.VMEM((2, 24, LANES), f32),
             pltpu.VMEM((2, CY - 8 + PY // 3, LANES), f32),
             pltpu.VMEM((2, CY - 8 + PY // 3, LANES), f32),
-            pltpu.VMEM((2, 2 * face, LANES), f32),
-            pltpu.VMEM((2, 2 * face, LANES), f32),
+            pltpu.VMEM((2, 8 * (CY + 2) // 3, LANES), f32),
+            pltpu.VMEM((2, 8 * (CY + 2) // 3, LANES), f32),
             pltpu.VMEM((4, 16, LANES), f32),
             pltpu.VMEM((4, 16, LANES), f32),
             pltpu.VMEM((2, 3 * PX + 2, LANES), f32),

time: 26.2 us -> 25.5 us (0.973)
  Pallas kernels: 25.4 us -> 24.8 us
    pallas_call x1, Pallas kernels: 22.9 us -> 22.3 us  [shards(): pl.pallas_call(deposit_kernel, name='deposit', out_shape=(grid_shape, rig...]
where the time goes in v8:
time: 25.5 us; the launch traced here: 25.4 us
  Pallas kernels  24.8 us (97%)
  between operations  0.64 us (3%)
    pallas_call x1, Pallas kernels, shards(): pl.pallas_call(deposit_kernel, name='deposit', out_shape=(grid_shape, rig...  22.3 us
    pallas_call x1, Pallas kernels, shards(): pl.pallas_call(collect_kernel, name='collect', out_shape=(jax.ShapeDtypeS...  2.51 us

profile of v8, /device:TPU:1, one launch (start us, length us, event | category | flops | bytes accessed | tf_op | source)
XLA Modules:
  0.0 25.4 jit_solution(2556433956003573245)
XLA Ops:
  0.6 22.3 %deposit.1 = (f32[1296,128]{1,0:T(8,128)S(1)}, bf16[1536,384]{1,0:T(8,128)(2,1)S(1)}, bf16[1536,384]{1,0:T(8,128)(2,1)S(1)}, f32[160,128]{1,0:T(8,128)S(1)}, f32[192,128]{1,0:T(8,128)S(1)}) custom-call(s32[32]{0:T(128)} %tile_hbm.3, s32[32]{0:T(128)} %count_hbm.1, f32[3,4096]{1,0:T(4,128)} %frac_hbm.1, s32[3,4096]{1,0:T(4,128)} %offset_hbm.1, ...), custom_call_target="tpu_custom_call" | custom-call | tf_op jit(solution)/shard_map/deposit/pallas_call | solution.py:869
  22.9 2.5 %collect.1 = (f32[3,4096]{1,0:T(4,128)}, f32[9,4096]{1,0:T(8,128)}, f32[6,4096]{1,0:T(8,128)}, f32[3,16,32,64]{3,2,1,0:T(8,128)}) custom-call(s32[32]{0:T(128)} %tile_hbm.3, f32[1296,128]{1,0:T(8,128)S(1)} %get-tuple-element.13.velocity, bf16[1536,384]{1,0:T(8,128)(2,1)S(1)} %get-tuple-element.14.right_high, ...), custom_call_target="tpu_custom_call" | custom-call | tf_op jit(solution)/shard_map/collect/pallas_call | solution.py:917

commit v9 on v8

--- a/solution.py
+++ b/solution.py
@@ -131,10 +131,11 @@
     collect_high,
     collect_low,
     y_table,
-    stress_out,
+    new_stress,
     mom,
     mass,
     shared_ref,
+    stress_out,
     tile_ref,
     count_ref,
     frac_ref,
@@ -643,6 +644,10 @@
         return carry
 
     lax.fori_loop(0, blocks // 2, right_sides, 0)
+    for block in range(blocks):
+        new_stress[:, block * BLOCK : (block + 1) * BLOCK] = stress_out[
+            pl.ds(block, 6, stride=blocks), :
+        ]
 
     for c in xz_copies:
         c.wait()
@@ -722,7 +727,6 @@
     new_stress_hbm,
     grid_velocity_hbm,
     tile_ref,
-    new_stress_ref,
     grid_velocity_ref,
     partial,
     final,
@@ -731,11 +735,7 @@
     blocks = tile_hbm.shape[0]
     tile_copy = pltpu.make_async_copy(tile_hbm, tile_ref, copy_sem.at[0])
     tile_copy.start()
-    for block in range(blocks):
-        new_stress_ref[:, block * BLOCK : (block + 1) * BLOCK] = stress_in[
-            pl.ds(block, 6, stride=blocks), :
-        ]
-    stress_copy = pltpu.make_async_copy(new_stress_ref, new_stress_hbm, copy_sem.at[1])
+    stress_copy = pltpu.make_async_copy(stress_in, new_stress_hbm, copy_sem.at[1])
     stress_copy.start()
     def output(step, carry):
         for member in range(4):
@@ -874,7 +874,7 @@
             right_shape,
             right_shape,
             jax.ShapeDtypeStruct((5 * blocks, LANES), f32),
-            jax.ShapeDtypeStruct((6 * blocks, LANES), f32),
+            jax.ShapeDtypeStruct((6, points), f32),
         ),
         in_specs=[hbm] * 8,
         out_specs=(vmem,) * 5,
@@ -882,6 +882,7 @@
             pltpu.VMEM((ROWS, LANES), f32),
             pltpu.VMEM((ROWS, LANES), f32),
             pltpu.VMEM((T_SHARED * blocks, LANES), f32),
+            pltpu.VMEM((6 * blocks, LANES), f32),
             pltpu.SMEM((blocks,), jnp.int32),
             pltpu.SMEM((blocks,), jnp.int32),
             pltpu.VMEM((3, points), f32),
@@ -927,7 +928,6 @@
         out_specs=(vmem, vmem, hbm, hbm),
         scratch_shapes=[
             pltpu.SMEM((blocks,), jnp.int32),
-            pltpu.VMEM((6, points), f32),
             pltpu.VMEM((3, CX, CZ, CY), f32),
             pltpu.VMEM((12 * 8 * blocks, LANES), f32),
             pltpu.VMEM((12 * blocks, LANES), f32),

time: 25.5 us -> 25.5 us (level)
  no operation moved by 1% of the time
where the time goes in v9:
time: 25.5 us; the launch traced here: 25.4 us
  Pallas kernels  24.8 us (97%)
  between operations  0.64 us (3%)
    pallas_call x1, Pallas kernels, shards(): pl.pallas_call(deposit_kernel, name='deposit', out_shape=(grid_shape, rig...  22.3 us
    pallas_call x1, Pallas kernels, shards(): pl.pallas_call(collect_kernel, name='collect', out_shape=(jax.ShapeDtypeS...  2.51 us

profile of v9, /device:TPU:1, one launch (start us, length us, event | category | flops | bytes accessed | tf_op | source)
XLA Modules:
  0.0 25.4 jit_solution(14158703851091320534)
XLA Ops:
  0.6 22.3 %deposit.1 = (f32[1296,128]{1,0:T(8,128)S(1)}, bf16[1536,384]{1,0:T(8,128)(2,1)S(1)}, bf16[1536,384]{1,0:T(8,128)(2,1)S(1)}, f32[160,128]{1,0:T(8,128)S(1)}, f32[6,4096]{1,0:T(8,128)S(1)}) custom-call(s32[32]{0:T(128)} %tile_hbm.3, s32[32]{0:T(128)} %count_hbm.1, f32[3,4096]{1,0:T(4,128)} %frac_hbm.1, s32[3,4096]{1,0:T(4,128)} %offset_hbm.1, ...), custom_call_target="tpu_custom_call" | custom-call | tf_op jit(solution)/shard_map/deposit/pallas_call | solution.py:869
  22.9 2.5 %collect.1 = (f32[3,4096]{1,0:T(4,128)}, f32[9,4096]{1,0:T(8,128)}, f32[6,4096]{1,0:T(8,128)}, f32[3,16,32,64]{3,2,1,0:T(8,128)}) custom-call(s32[32]{0:T(128)} %tile_hbm.3, f32[1296,128]{1,0:T(8,128)S(1)} %get-tuple-element.13.velocity, bf16[1536,384]{1,0:T(8,128)(2,1)S(1)} %get-tuple-element.14.right_high, ...), custom_call_target="tpu_custom_call" | custom-call | tf_op jit(solution)/shard_map/collect/pallas_call | solution.py:918
